TPU v7x, 128 devices: a whole 4x4x4 slice. The times are simulated.
128 devices in a mesh: polar: 16 (over x_hi, y, core), azimuth: 8 (over x_lo, z).
Axes of the slice: x: 4 (x_hi: 2, x_lo: 2; x = x_hi * 2 + x_lo), y: 4, z: 4, core: 2. Of those that a mesh axis runs over, the one named last changes fastest.
Arguments:
- grid_input: bfloat16 [720, 276480], P('polar', 'azimuth'), may hold values from -6 to 6
- cotangent: bfloat16 [720, 192, 1440], P('polar', 'azimuth'), may hold values from -6 to 6
- forward_legendre: bfloat16 [720, 256, 256], P(None, 'polar'), may hold values from -0.21875 to 0.21875
- inverse_legendre: bfloat16 [720, 256, 256], P(None, 'polar'), may hold values from -0.375 to 0.375
- filter_weight: bfloat16 [256, 73728], P('polar'), may hold values from -0.3125 to 0.3125
Outputs:
- filtered: bfloat16 [720, 192, 1440], P('polar', 'azimuth')
- grid_grad: bfloat16 [720, 276480], P('polar', 'azimuth')
All inputs are finite; a program needn't handle non-finite values.
Results may differ from a plain program's by a relative error of at most 0.02.
Values may be sent and summed in bfloat16 or wider, within the bound.
No kernel may reach another device: no remote copies, remote signals or barrier semaphores. Data moves between devices by JAX's collectives and lax.ppermute only.
A program may use at most 256 MiB of HBM per device.

v0:
```python
import math

import jax
import jax.numpy as jnp
from jax import lax
from jax.sharding import PartitionSpec as P

LON = 1440
C = 192
ORDERS = 256


def make_tables():
    longitude = jnp.arange(LON, dtype=jnp.int32)
    order_index = jnp.arange(ORDERS, dtype=jnp.int32)
    phases = (longitude[:, None] * order_index[None, :] % LON).astype(jnp.float32)
    angles = phases * (2.0 * math.pi / LON)
    factor = 1.0 / math.sqrt(LON)
    stacked = jnp.stack([jnp.cos(angles) * factor, -jnp.sin(angles) * factor], axis=-1)
    doubling = jnp.where(order_index == 0, 1.0, 2.0).astype(jnp.float32)
    basis_plain = stacked.reshape(LON, 2 * ORDERS).astype(jnp.bfloat16)
    basis_doubled = (
        (stacked * doubling[None, :, None]).reshape(LON, 2 * ORDERS).astype(jnp.bfloat16)
    )
    return (basis_plain, basis_doubled)


def to_spectrum(segment, basis_plain):
    product = jnp.einsum("alc,lj->ajc", segment, basis_plain, preferred_element_type=jnp.float32)
    return product.astype(jnp.bfloat16).reshape(segment.shape[0], ORDERS, 2, segment.shape[2])


def mix_forward(modes, kernel):
    shape_in = modes.shape
    flat = modes.reshape(shape_in[0], shape_in[1], 2 * shape_in[3])
    result = jnp.einsum("lmk,lkj->lmj", flat, kernel, preferred_element_type=jnp.float32)
    return result.astype(jnp.bfloat16).reshape(shape_in)


def mix_adjoint(modes, kernel):
    shape_in = modes.shape
    flat = modes.reshape(shape_in[0], shape_in[1], 2 * shape_in[3])
    result = jnp.einsum("lmj,lkj->lmk", flat, kernel, preferred_element_type=jnp.float32)
    return result.astype(jnp.bfloat16).reshape(shape_in)


def to_modes(coefficients):
    return lax.all_to_all(coefficients, "azimuth", split_axis=1, concat_axis=3, tiled=True)


def from_modes(mixed_modes):
    return lax.all_to_all(mixed_modes, "azimuth", split_axis=3, concat_axis=1, tiled=True)


def degree_sum_local(field, table):
    columns = lax.all_to_all(field, "polar", split_axis=1, concat_axis=0, tiled=True)
    blocks = lax.axis_size("polar")
    row_count = columns.shape[0] // blocks
    split_field = columns.reshape(blocks, row_count, columns.shape[1], 2, columns.shape[3])
    split_table = table.reshape(blocks, row_count, table.shape[1], table.shape[2])
    partial_sums = jnp.einsum(
        "bamrc,baml->blmrc", split_field, split_table, preferred_element_type=jnp.float32
    )
    rounded = lax.optimization_barrier(partial_sums.astype(jnp.bfloat16))
    summed = jnp.sum(rounded.astype(jnp.float32), axis=0).astype(jnp.bfloat16)
    return lax.all_to_all(summed, "polar", split_axis=0, concat_axis=1, tiled=True)


def degree_rows_local(modes, table):
    all_degrees = lax.all_to_all(modes, "polar", split_axis=1, concat_axis=0, tiled=True)
    grid_rows = jnp.einsum(
        "lmrc,aml->amrc", all_degrees, table, preferred_element_type=jnp.float32
    ).astype(jnp.bfloat16)
    return lax.all_to_all(grid_rows, "polar", split_axis=0, concat_axis=1, tiled=True)


def on_device(grid_input, cotangent, forward_legendre, inverse_legendre, filter_weight):
    basis_plain, basis_doubled = make_tables()
    weight_cube = filter_weight.reshape(filter_weight.shape[0], 2, C, C)
    weight_real = weight_cube[:, 0]
    weight_imag = weight_cube[:, 1]
    upper_rows = jnp.concatenate([weight_real, weight_imag], axis=2)
    lower_rows = jnp.concatenate([-weight_imag, weight_real], axis=2)
    kernel = jnp.concatenate([upper_rows, lower_rows], axis=1)
    grid_cube = grid_input.reshape(grid_input.shape[0], grid_input.shape[1] // C, C)
    spectrum = (lambda segment: to_spectrum(segment, basis_plain))(
        lax.all_to_all(grid_cube, "azimuth", split_axis=2, concat_axis=1, tiled=True)
    )
    lat_rows = cotangent.shape[0]
    chan_rows = cotangent.shape[1]
    grad_synthesis = jnp.einsum(
        "acl,lj->ajc", cotangent, basis_doubled, preferred_element_type=jnp.float32
    )
    grad_synthesis = grad_synthesis.astype(jnp.bfloat16).reshape(lat_rows, ORDERS, 2, chan_rows)
    coefficients = degree_sum_local(spectrum, forward_legendre)
    grad_mixed = degree_sum_local(grad_synthesis, inverse_legendre)
    mixed_modes = from_modes(mix_forward(to_modes(coefficients), kernel))
    grad_coefficients = from_modes(mix_adjoint(to_modes(grad_mixed), kernel))
    synthesis = degree_rows_local(mixed_modes, inverse_legendre)
    grad_spectrum = degree_rows_local(grad_coefficients, forward_legendre)
    filtered = jnp.einsum(
        "ajc,lj->acl",
        synthesis.reshape(lat_rows, 2 * ORDERS, chan_rows),
        basis_doubled,
        preferred_element_type=jnp.float32,
    ).astype(jnp.bfloat16)
    grad_full = jnp.einsum(
        "ajc,lj->alc",
        grad_spectrum.reshape(lat_rows, 2 * ORDERS, chan_rows),
        basis_plain,
        preferred_element_type=jnp.float32,
    ).astype(jnp.bfloat16)
    grid_grad = lax.all_to_all(grad_full, "azimuth", split_axis=1, concat_axis=2, tiled=True)
    return (
        filtered,
        grid_grad.reshape(grid_grad.shape[0], grid_grad.shape[1] * grid_grad.shape[2]),
    )


def solution(mesh):
    return jax.shard_map(
        on_device,
        mesh=mesh,
        in_specs=(
            P("polar", "azimuth"),
            P("polar", "azimuth", None),
            P(None, "polar", None),
            P(None, "polar", None),
            P("polar", None),
        ),
        out_specs=(P("polar", "azimuth", None), P("polar", "azimuth")),
        check_vma=False,
    )
```

profile of v0, /device:TPU:1, one launch (start us, length us, event | category | flops | bytes accessed | tf_op | source)
XLA Modules:
  0.0 646.1 jit_solution(9863970102031459745)
XLA Ops:
  0.7 7.9 %negate_multiply_fusion = (f32[1440,256,1]{1,0,2:T(8,128)}, f32[1440,256,1]{1,0,2:T(8,128)}) fusion(), kind=kLoop, calls=%fused_computation.39 | loop fusion | flops 4423680 | bytes 2949120 | tf_op jit(solution)/shard_map/mul | solution.py:19
  39.3 27.3 %all_to_all.231 = bf16[16,2,17280]{2,1,0:T(2,128)(2,1)} all-to-all(bf16[16,2,17280]{2,1,0:T(2,128)(2,1)} %reshape.198), channel_id=1, replica_groups=mesh['polar'=16,'azimuth'=8] {'polar'}, dimensions={0} | all-to-all | bytes 2211840 | tf_op jit(solution)/shard_map/all_to_all | solution.py:56
  66.7 9.4 %reshape.199 = bf16[256,2,24,45]{3,2,1,0:T(8,128)(2,1)S(1)} reshape(bf16[16,2,17280]{2,1,0:T(2,128)(2,1)} %all_to_all.231) | data formatting | bytes 2211840
  76.0 7.9 %convert_bitcast_fusion = bf16[16,256,16,2,24]{1,4,3,2,0:T(8,128)(2,1)} fusion(bf16[16,45,16,2,24]{1,4,3,2,0:T(8,128)(2,1)S(1)} %bitcast.176, bf16[16,45,16,256,1]{3,2,1,0,4:T(8,128)(2,1)} %bitcast.162), kind=kOutput, calls=%fused_computation.4 | convolution fusion | flops 286261248 | bytes 13295616 | tf_op jit(solution)/shard_map/bamrc,baml->blmrc/dot_general | solution.py:61
  92.3 12.8 %all_to_all.232 = bf16[16,2,6144]{2,1,0:T(2,128)(2,1)S(1)} all-to-all(bf16[16,2,6144]{2,1,0:T(2,128)(2,1)S(1)} %reshape.200), channel_id=1, replica_groups=mesh['polar'=16,'azimuth'=8] {'polar'}, dimensions={0} | all-to-all | bytes 786432 | tf_op jit(solution)/shard_map/all_to_all | solution.py:66
  129.4 6.9 %reshape.164 = bf16[45,180,192]{2,1,0:T(8,128)(2,1)} reshape(bf16[45,34560]{1,0:T(8,128)(2,1)} %param.5) | data formatting | bytes 6220800 | tf_op jit(solution)/shard_map/reshape | solution.py:85
  136.3 7.6 %copy.181 = bf16[45,180,192]{1,0,2:T(8,128)(2,1)} copy(bf16[45,180,192]{2,1,0:T(8,128)(2,1)} %reshape.164) | data formatting | bytes 6220800 | tf_op jit(solution)/shard_map/reshape | solution.py:85
  185.9 18.0 %all-to-all-done = bf16[45,180,192]{1,0,2:T(8,128)(2,1)} async-done(((bf16[45,180,192]{1,0,2:T(8,128)(2,1)}), bf16[45,180,192]{1,0,2:T(8,128)(2,1)}, u32[]{:S(2)}, u32[]{:S(2)}) %all-to-all-start) | async-done | bytes 3110432 | tf_op jit(solution)/shard_map/all_to_all | solution.py:87
  208.2 7.0 %copy.244 = bf16[45,8,180,24]{2,1,0,3:T(8,128)(2,1)} copy(bf16[45,8,180,24]{2,0,3,1:T(8,128)(2,1)} %bitcast.3) | data formatting | bytes 6220800 | tf_op jit(solution)/shard_map/all_to_all | solution.py:87
  215.1 9.1 %reshape.185 = bf16[45,1440,24]{1,0,2:T(8,128)(2,1)} reshape(bf16[45,8,180,24]{2,1,0,3:T(8,128)(2,1)} %copy.244) | data formatting | bytes 6220800 | tf_op jit(solution)/shard_map/all_to_all | solution.py:87
  233.1 6.4 reshape.186
  268.9 9.4 %reshape.187 = bf16[256,2,24,45]{3,2,1,0:T(8,128)(2,1)S(1)} reshape(bf16[16,2,17280]{2,1,0:T(2,128)(2,1)} %copy-done.5) | data formatting | bytes 2211840
  278.3 7.9 %convert_bitcast_fusion.1 = bf16[16,256,16,2,24]{1,4,3,2,0:T(8,128)(2,1)} fusion(bf16[16,45,16,2,24]{1,4,3,2,0:T(8,128)(2,1)S(1)} %bitcast.177, bf16[16,45,16,256,1]{3,2,1,0,4:T(8,128)(2,1)} %bitcast.160), kind=kOutput, calls=%fused_computation.5 | convolution fusion | flops 286261248 | bytes 13295616 | tf_op jit(solution)/shard_map/bamrc,baml->blmrc/dot_general | solution.py:61
  295.2 7.6 %all-to-all-start.2 = ((bf16[16,2,6144]{2,1,0:T(2,128)(2,1)}), bf16[16,2,6144]{2,1,0:T(2,128)(2,1)}, u32[]{:S(2)}, u32[]{:S(2)}) async-start(bf16[16,2,6144]{2,1,0:T(2,128)(2,1)} %reshape.188), calls=%async_computation.2 | async-start | bytes 786432 | tf_op jit(solution)/shard_map/all_to_all | solution.py:66
  302.8 8.5 %reshape.207 = bf16[256,16,2,24]{3,2,1,0:T(2,128)(2,1)} reshape(bf16[16,2,6144]{2,1,0:T(2,128)(2,1)} %all-to-all-done.11) | data formatting | bytes 786432
  321.0 8.4 %reshape.189 = bf16[256,16,2,24]{3,2,1,0:T(2,128)(2,1)} reshape(bf16[16,2,6144]{2,1,0:T(2,128)(2,1)} %all-to-all-done.2) | data formatting | bytes 786432
  356.1 8.3 %copy.226 = bf16[720,16,2,24]{3,2,1,0:T(2,128)(2,1)} copy(bf16[720,16,2,24]{0,3,2,1:T(8,128)(2,1)S(1)} %fusion.42) | data formatting | bytes 2211840 | tf_op jit(solution)/shard_map/convert_element_type | solution.py:73
  364.3 19.5 %reshape.208 = bf16[16,2,17280]{2,1,0:T(2,128)(2,1)} reshape(bf16[720,16,2,24]{3,2,1,0:T(2,128)(2,1)} %copy.226) | data formatting | bytes 2211840
  384.6 8.5 %all-to-all-start.12 = ((bf16[16,2,17280]{2,1,0:T(2,128)(2,1)}), bf16[16,2,17280]{2,1,0:T(2,128)(2,1)S(1)}, u32[]{:S(2)}, u32[]{:S(2)}) async-start(bf16[16,2,17280]{2,1,0:T(2,128)(2,1)} %reshape.208), calls=%async_computation.12 | async-start | bytes 2211840 | tf_op jit(solution)/shard_map/all_to_all | solution.py:74
  419.4 9.4 %reshape.209 = bf16[720,16,2,24]{3,2,1,0:T(2,128)(2,1)} reshape(bf16[16,2,17280]{2,1,0:T(2,128)(2,1)S(1)} %all-to-all-done.12) | data formatting | bytes 2211840
  428.8 16.3 %copy.227 = bf16[16,45,16,2,24]{1,4,3,2,0:T(8,128)(2,1)} copy(bf16[16,45,16,2,24]{4,3,2,1,0:T(2,128)(2,1)} %bitcast.167) | data formatting | bytes 2211840 | tf_op jit(solution)/shard_map/all_to_all | solution.py:74
  456.8 8.1 %all-to-all-start.5 = ((bf16[16,2,6144]{2,1,0:T(2,128)(2,1)}), bf16[16,2,6144]{2,1,0:T(2,128)(2,1)S(1)}, u32[]{:S(2)}, u32[]{:S(2)}) async-start(bf16[16,2,6144]{2,1,0:T(2,128)(2,1)} %reshape.194), calls=%async_computation.5 | async-start | bytes 786432 | tf_op jit(solution)/shard_map/all_to_all | solution.py:70
  471.3 10.9 %copy.230 = bf16[45,1440,24]{0,2,1:T(8,128)(2,1)} copy(bf16[45,1440,24]{1,0,2:T(8,128)(2,1)} %fusion.14) | data formatting | bytes 6220800 | tf_op jit(solution)/shard_map/convert_element_type | solution.py:112
  482.2 14.4 %reshape.210 = bf16[8,2,97200]{2,1,0:T(2,128)(2,1)} reshape(bf16[1440,24,45]{2,1,0:T(8,128)(2,1)} %bitcast.164) | data formatting | bytes 6220800
  521.5 8.3 %copy.203 = bf16[720,16,2,24]{3,2,1,0:T(2,128)(2,1)} copy(bf16[720,16,2,24]{0,3,2,1:T(8,128)(2,1)S(1)} %fusion.45) | data formatting | bytes 2211840 | tf_op jit(solution)/shard_map/convert_element_type | solution.py:73
  529.8 19.6 %reshape.196 = bf16[16,2,17280]{2,1,0:T(2,128)(2,1)} reshape(bf16[720,16,2,24]{3,2,1,0:T(2,128)(2,1)} %copy.203) | data formatting | bytes 2211840
  549.4 8.4 %all-to-all-start.6 = ((bf16[16,2,17280]{2,1,0:T(2,128)(2,1)}), bf16[16,2,17280]{2,1,0:T(2,128)(2,1)}, u32[]{:S(2)}, u32[]{:S(2)}) async-start(bf16[16,2,17280]{2,1,0:T(2,128)(2,1)} %reshape.196), calls=%async_computation.6 | async-start | bytes 2211840 | tf_op jit(solution)/shard_map/all_to_all | solution.py:74
  561.9 17.6 %reshape.211 = bf16[1440,24,45]{2,1,0:T(8,128)(2,1)} reshape(bf16[8,2,97200]{2,1,0:T(2,128)(2,1)} %all-to-all-done.13) | data formatting | bytes 6220800
  579.5 9.5 %copy.232 = bf16[45,180,8,24]{0,3,2,1:T(8,128)(2,1)} copy(bf16[45,180,8,24]{0,3,1,2:T(8,128)(2,1)} %bitcast.165) | data formatting | bytes 6220800 | tf_op jit(solution)/shard_map/all_to_all | solution.py:113
  589.0 8.8 %copy.233 = bf16[45,34560]{1,0:T(8,128)(2,1)} copy(bf16[45,34560]{0,1:T(8,128)(2,1)} %bitcast.166) | data formatting | bytes 6220800
  597.8 20.8 %reshape.197 = bf16[720,16,2,24]{3,2,1,0:T(2,128)(2,1)} reshape(bf16[16,2,17280]{2,1,0:T(2,128)(2,1)} %all-to-all-done.6) | data formatting | bytes 2211840
  618.6 16.3 %copy.204 = bf16[16,45,16,2,24]{1,4,3,2,0:T(8,128)(2,1)} copy(bf16[16,45,16,2,24]{4,3,2,1,0:T(2,128)(2,1)} %bitcast.168) | data formatting | bytes 2211840 | tf_op jit(solution)/shard_map/all_to_all | solution.py:74
  (101 shorter events, 278.1 us)
Async XLA Ops:
  0.6 23.4 %copy-start = (bf16[45,24,1440]{2,1,0:T(8,128)(2,1)S(1)}, bf16[45,24,1440]{2,1,0:T(8,128)(2,1)}, u32[]{:S(2)}) copy-start(bf16[45,24,1440]{2,1,0:T(8,128)(2,1)} %param.6) | copy-start | bytes 9331204
  124.3 19.6 %all-to-all-start.9 = ((bf16[8,2,12288]{2,1,0:T(2,128)(2,1)}), bf16[8,2,12288]{2,1,0:T(2,128)(2,1)}, u32[]{:S(2)}, u32[]{:S(2)}) async-start(bf16[8,2,12288]{2,1,0:T(2,128)(2,1)} %reshape.202), calls=%async_computation.9 | async-start | bytes 786432 | tf_op jit(solution)/shard_map/all_to_all | solution.py:48
  143.9 5.7 copy-start.2
  143.9 5.7 copy-start.3
  143.9 60.0 %all-to-all-start = ((bf16[45,180,192]{1,0,2:T(8,128)(2,1)}), bf16[45,180,192]{1,0,2:T(8,128)(2,1)}, u32[]{:S(2)}, u32[]{:S(2)}) async-start(bf16[45,180,192]{1,0,2:T(8,128)(2,1)} %copy.181), calls=%async_computation | async-start | bytes 9437184 | tf_op jit(solution)/shard_map/all_to_all | solution.py:87
  203.9 35.6 %all-to-all-start.10 = ((bf16[8,2,12288]{2,1,0:T(2,128)(2,1)}), bf16[8,2,12288]{2,1,0:T(2,128)(2,1)}, u32[]{:S(2)}, u32[]{:S(2)}) async-start(bf16[8,2,12288]{2,1,0:T(2,128)(2,1)} %reshape.204), calls=%async_computation.10 | async-start | bytes 786432 | tf_op jit(solution)/shard_map/all_to_all | solution.py:52
  215.1 9.1 %copy-start.7 = (bf16[1440,512]{0,1:T(8,128)(2,1)S(1)}, bf16[1440,512]{0,1:T(8,128)(2,1)}, u32[]{:S(2)}) copy-start(bf16[1440,512]{0,1:T(8,128)(2,1)} %convert_element_type.103) | copy-start | bytes 4423684
  239.5 22.9 %all-to-all-start.1 = ((bf16[16,2,17280]{2,1,0:T(2,128)(2,1)}), bf16[16,2,17280]{2,1,0:T(2,128)(2,1)S(1)}, u32[]{:S(2)}, u32[]{:S(2)}) async-start(bf16[16,2,17280]{2,1,0:T(2,128)(2,1)} %reshape.186), calls=%async_computation.1 | async-start | bytes 2211840 | tf_op jit(solution)/shard_map/all_to_all | solution.py:56
  262.4 1.0 copy-start.5
  263.4 31.8 %all-to-all-start.11 = ((bf16[16,2,6144]{2,1,0:T(2,128)(2,1)}), bf16[16,2,6144]{2,1,0:T(2,128)(2,1)}, u32[]{:S(2)}, u32[]{:S(2)}) async-start(bf16[16,2,6144]{2,1,0:T(2,128)(2,1)} %reshape.206), calls=%async_computation.11 | async-start | bytes 786432 | tf_op jit(solution)/shard_map/all_to_all | solution.py:70
  295.2 25.8 %all-to-all-start.2 = ((bf16[16,2,6144]{2,1,0:T(2,128)(2,1)}), bf16[16,2,6144]{2,1,0:T(2,128)(2,1)}, u32[]{:S(2)}, u32[]{:S(2)}) async-start(bf16[16,2,6144]{2,1,0:T(2,128)(2,1)} %reshape.188), calls=%async_computation.2 | async-start | bytes 786432 | tf_op jit(solution)/shard_map/all_to_all | solution.py:66
  340.1 9.8 %copy-start.6 = (bf16[256,16,2,24]{0,3,2,1:T(8,128)(2,1)S(1)}, bf16[256,16,2,24]{0,3,2,1:T(8,128)(2,1)}, u32[]{:S(2)}) copy-start(bf16[256,16,2,24]{0,3,2,1:T(8,128)(2,1)} %all_to_all.210) | copy-start | bytes 1179652
  344.8 39.0 %all-to-all-start.3 = ((bf16[8,2,12288]{2,1,0:T(2,128)(2,1)}), bf16[8,2,12288]{2,1,0:T(2,128)(2,1)S(1)}, u32[]{:S(2)}, u32[]{:S(2)}) async-start(bf16[8,2,12288]{2,1,0:T(2,128)(2,1)} %reshape.190), calls=%async_computation.3 | async-start | bytes 786432 | tf_op jit(solution)/shard_map/all_to_all | solution.py:48
  383.8 0.7 copy-start.8
  384.6 29.5 %all-to-all-start.12 = ((bf16[16,2,17280]{2,1,0:T(2,128)(2,1)}), bf16[16,2,17280]{2,1,0:T(2,128)(2,1)S(1)}, u32[]{:S(2)}, u32[]{:S(2)}) async-start(bf16[16,2,17280]{2,1,0:T(2,128)(2,1)} %reshape.208), calls=%async_computation.12 | async-start | bytes 2211840 | tf_op jit(solution)/shard_map/all_to_all | solution.py:74
  414.1 31.0 %all-to-all-start.4 = ((bf16[8,2,12288]{2,1,0:T(2,128)(2,1)}), bf16[8,2,12288]{2,1,0:T(2,128)(2,1)S(1)}, u32[]{:S(2)}, u32[]{:S(2)}) async-start(bf16[8,2,12288]{2,1,0:T(2,128)(2,1)} %reshape.192), calls=%async_computation.4 | async-start | bytes 786432 | tf_op jit(solution)/shard_map/all_to_all | solution.py:52
  456.8 39.7 %all-to-all-start.5 = ((bf16[16,2,6144]{2,1,0:T(2,128)(2,1)}), bf16[16,2,6144]{2,1,0:T(2,128)(2,1)S(1)}, u32[]{:S(2)}, u32[]{:S(2)}) async-start(bf16[16,2,6144]{2,1,0:T(2,128)(2,1)} %reshape.194), calls=%async_computation.5 | async-start | bytes 786432 | tf_op jit(solution)/shard_map/all_to_all | solution.py:70
  496.6 52.8 %all-to-all-start.13 = ((bf16[8,2,97200]{2,1,0:T(2,128)(2,1)}), bf16[8,2,97200]{2,1,0:T(2,128)(2,1)}, u32[]{:S(2)}, u32[]{:S(2)}) async-start(bf16[8,2,97200]{2,1,0:T(2,128)(2,1)} %reshape.210), calls=%async_computation.13 | async-start | bytes 6225920 | tf_op jit(solution)/shard_map/all_to_all | solution.py:113
  529.8 28.1 %copy-start.4 = (bf16[1440,256,2]{1,0,2:T(8,128)(2,1)S(1)}, bf16[1440,256,2]{1,0,2:T(8,128)(2,1)}, u32[]{:S(2)}) copy-start(bf16[1440,256,2]{1,0,2:T(8,128)(2,1)} %get-tuple-element.15) | copy-start | bytes 4423684
  549.4 48.4 %all-to-all-start.6 = ((bf16[16,2,17280]{2,1,0:T(2,128)(2,1)}), bf16[16,2,17280]{2,1,0:T(2,128)(2,1)}, u32[]{:S(2)}, u32[]{:S(2)}) async-start(bf16[16,2,17280]{2,1,0:T(2,128)(2,1)} %reshape.196), calls=%async_computation.6 | async-start | bytes 2211840 | tf_op jit(solution)/shard_map/all_to_all | solution.py:74
  634.9 11.0 %copy-start.1 = (bf16[45,24,1440]{2,1,0:T(8,128)(2,1)S(1)}, bf16[45,24,1440]{2,1,0:T(8,128)(2,1)}, u32[]{:S(2)}) copy-start(bf16[45,24,1440]{2,1,0:T(8,128)(2,1)} %param.6) | copy-start | bytes 9331204
where the time goes:
time: 656 us; the launch traced here: 646 us
  local copies, waits for them, and re-layouts  429 us (65%)
  starting transfers between devices  73.9 us (11%)
  matrix products  59 us (9%)
  blocking collectives  40.2 us (6%)
  other arithmetic  22.4 us (3%)
  waiting for transfers between devices  20.7 us (3%)
    unnamed x45, local copies, waits for them, and re-layouts  207 us
    all_to_all x2, local copies, waits for them, and re-layouts, degree_rows_local(): lax.all_to_all(grid_rows, 'polar', split_axis=0, concat_axis=1, tiled=True)  32.6 us
    all_to_all x1, blocking collectives, degree_sum_local(): lax.all_to_all(field, 'polar', split_axis=1, concat_axis=0, tiled=True)  27.3 us
    all_to_all x4, local copies, waits for them, and re-layouts, degree_sum_local(): lax.all_to_all(summed, 'polar', split_axis=0, concat_axis=1, tiled=True)  21.4 us
    all_to_all x4, local copies, waits for them, and re-layouts, degree_rows_local(): lax.all_to_all(modes, 'polar', split_axis=1, concat_axis=0, tiled=True)  19.5 us
    all_to_all x1, waiting for transfers between devices, on_device(): lax.all_to_all(grid_cube, 'azimuth', split_axis=2, concat_axis=1, tiled=T...  18 us
    all_to_all x2, starting transfers between devices, degree_rows_local(): lax.all_to_all(grid_rows, 'polar', split_axis=0, concat_axis=1, tiled=True)  16.9 us
    convert_element_type x2, local copies, waits for them, and re-layouts, degree_rows_local(): grid_rows = jnp.einsum('lmrc,aml->amrc', all_degrees, table, preferred_el...  16.5 us
  transfers between devices with their start and end apart: 12, of which 2 were waited for; matrix products, arithmetic and copies ran while one was open for 52% of the time, Pallas kernels for 0%

commit v1 on v0

v1 whole, which is shorter than its diff:
```python
import functools
import math
import numpy as np
import ml_dtypes
import jax
import jax.numpy as jnp
from jax import lax
from jax.sharding import PartitionSpec as P
from jax.experimental import pallas as pl
from jax.experimental.pallas import tpu as pltpu

LAT = 720
LON = 1440
C = 192
DEG = 256
ORD = 256
NP = 16
NA = 8
ROWS = 45
SLOTS = 6
PAIRS = 90
LP = 96
W = 1152
F32 = jnp.float32
BF = jnp.bfloat16


def params():
    return pltpu.CompilerParams(vmem_limit_bytes=56 << 20)


def dot(a, b, ca, cb):
    return lax.dot_general(a, b, (((ca,), (cb,)), ((), ())), preferred_element_type=F32)


def tables():
    lon = np.arange(LON)[:, None]
    m = np.arange(ORD)[None, :]
    ang = ((lon * m) % LON) * (2.0 * math.pi / LON)
    fac = 1.0 / math.sqrt(LON)
    st = np.stack([np.cos(ang) * fac, -np.sin(ang) * fac], axis=-1).astype(np.float32)
    dbl = np.where(np.arange(ORD) == 0, 1.0, 2.0).astype(np.float32)[None, :, None]
    plain = st.reshape(LON, 2 * ORD).astype(ml_dtypes.bfloat16)
    doubled = (st * dbl).reshape(LON, 2 * ORD).astype(ml_dtypes.bfloat16)
    p4 = plain.reshape(NA, PAIRS, 2, 2 * ORD).transpose(2, 0, 1, 3)
    pp = np.zeros((2, NA, LP, 2 * ORD), ml_dtypes.bfloat16)
    pp[:, :, :PAIRS] = p4
    pp = pp.reshape(2 * NA * LP, 2 * ORD)
    return np.ascontiguousarray(doubled.T), np.ascontiguousarray(pp.T), pp


def prep_body(x_ref, o_ref, s_ref):
    step = pl.program_id(0)
    lane = lax.broadcasted_iota(jnp.int32, (8, 6144), 1) + step * 6144
    good = lane < PAIRS * 384
    for k in range(SLOTS):
        if k < 5:
            v = x_ref[8 * k:8 * k + 8, :].astype(F32)
        else:
            v = jnp.concatenate([x_ref[40:45, :].astype(F32), jnp.zeros((3, 6144), F32)], 0)
        v = jnp.where(good, v, 0.0)
        for lp in range(16):
            for t in range(3):
                s_ref[3 * k + t, pl.ds(lp, 8, stride=16), :] = v[:, (3 * lp + t) * 128:(3 * lp + t + 1) * 128]
    for a in range(NA):
        for q in range(18):
            o_ref[a, :, q * 128:(q + 1) * 128] = s_ref[q, 16 * a:16 * a + 16, :].astype(BF)


def prep(x):
    return pl.pallas_call(
        prep_body,
        grid=(6,),
        out_shape=jax.ShapeDtypeStruct((NA, LP, 2304), BF),
        in_specs=[pl.BlockSpec((ROWS, 6144), lambda i: (0, i))],
        out_specs=pl.BlockSpec((NA, 16, 2304), lambda i: (0, i, 0)),
        scratch_shapes=[pltpu.VMEM((18, 128, 128), F32)],
        compiler_params=params(),
        name="prep",
    )(x)


def post_body(r_ref, o_ref, s_ref):
    for a in range(NA):
        for q in range(18):
            s_ref[q, 16 * a:16 * a + 16, :] = r_ref[a, :, q * 128:(q + 1) * 128].astype(F32)
    for k in range(SLOTS):
        for lp in range(16):
            for t in range(3):
                v = s_ref[3 * k + t, pl.ds(lp, 8, stride=16), :].astype(BF)
                n = 8 if k < 5 else 5
                o_ref[8 * k:8 * k + n, (3 * lp + t) * 128:(3 * lp + t + 1) * 128] = v[:n]


def post(r):
    return pl.pallas_call(
        post_body,
        grid=(6,),
        out_shape=jax.ShapeDtypeStruct((ROWS, LON // NA * C), BF),
        in_specs=[pl.BlockSpec((NA, 16, 2304), lambda i: (0, i, 0))],
        out_specs=pl.BlockSpec((ROWS, 6144), lambda i: (0, i)),
        scratch_shapes=[pltpu.VMEM((18, 128, 128), F32)],
        compiler_params=params(),
        name="post",
    )(r)


def whole(body, out, *args, scratch=(), name=None):
    return pl.pallas_call(
        body,
        out_shape=jax.ShapeDtypeStruct(out, BF),
        scratch_shapes=list(scratch),
        compiler_params=params(),
        name=name,
    )(*args)


def dft_f_body(r_ref, b_ref, o_ref, x_ref):
    for k in range(SLOTS):
        v = r_ref[:, :, 384 * k:384 * k + 384].reshape(NA * LP, 384)
        x_ref[0:768, C * k:C * k + C] = v[:, :C]
        x_ref[768:1536, C * k:C * k + C] = v[:, C:]
    y = dot(b_ref[...], x_ref[...], 1, 0).astype(BF)
    o_ref[...] = y.reshape(128, 4, W)


def dft_f(r, bpt):
    return whole(dft_f_body, (128, 4, W), r, bpt, scratch=[pltpu.VMEM((1536, W), BF)], name="dft_f")


def dft_g_body(x_ref, b_ref, o_ref):
    y = dot(b_ref[...], x_ref[...], 1, 1).astype(BF)
    y = jnp.concatenate([y, jnp.zeros((512, W - 1080), BF)], 1)
    o_ref[...] = y.reshape(128, 4, W)


def dft_g(x, bdt):
    return whole(dft_g_body, (128, 4, W), x, bdt, name="dft_g")


def leg_f_body(r_ref, p_ref, o_ref, s_ref):
    for m in range(2):
        for r in range(2):
            v = r_ref[:, 2 * m + r, :]
            for k in range(SLOTS):
                s_ref[128 * k:128 * k + 128, C * r:C * r + C] = v[:, C * k:C * k + C]
        y = dot(p_ref[m], s_ref[...], 0, 0).astype(BF)
        o_ref[:, 384 * m:384 * m + 384] = y


def leg_f(r, pf):
    return whole(leg_f_body, (DEG, 768), r, pf, scratch=[pltpu.VMEM((768, 384), BF)], name="leg_f")


def leg_g_body(r_ref, p_ref, o_ref, s_ref):
    for m in range(2):
        for r in range(2):
            v = r_ref[:, 2 * m + r, :].astype(F32).reshape(NP, NA, W)
            for a in range(NA):
                va = v[:, a, :].astype(BF)
                for t in range(48):
                    s_ref[16 * t:16 * t + 16, C * r + 24 * a:C * r + 24 * a + 24] = va[:, 24 * t:24 * t + 24]
        y = dot(p_ref[m], s_ref[...], 0, 0).astype(BF)
        o_ref[:, 384 * m:384 * m + 384] = y


def leg_g(r, pi):
    return whole(leg_g_body, (DEG, 768), r, pi, scratch=[pltpu.VMEM((768, 384), BF)], name="leg_g")


def mix_body(adjoint, r_ref, k_ref, o_ref, s_ref):
    i = lax.broadcasted_iota(jnp.int32, (256, 256), 0)
    j = lax.broadcasted_iota(jnp.int32, (256, 256), 1)
    perm = ((i // 16 == j % 16) & (i % 16 == j // 16)).astype(F32).astype(BF)
    x = dot(perm, r_ref[...].reshape(256, 768), 1, 0).astype(BF)
    for l in range(16):
        v = x[16 * l:16 * l + 16]
        v = jnp.concatenate([v[:, :384], v[:, 384:]], 0)
        y = dot(v, k_ref[l], 1, 1 if adjoint else 0).astype(BF)
        s_ref[16 * l:16 * l + 16, :384] = y[:16]
        s_ref[16 * l:16 * l + 16, 384:] = y[16:]
    o_ref[...] = dot(perm, s_ref[...], 1, 0).astype(BF).reshape(16, 16, 768)


def mix(r, k, adjoint):
    return whole(functools.partial(mix_body, adjoint), (16, 16, 768), r, k, scratch=[pltpu.VMEM((256, 768), BF)], name="mix_g" if adjoint else "mix_f")


def syn_f_body(x_ref, p_ref, o_ref, z_ref):
    for m in range(2):
        y = dot(p_ref[m], x_ref[:, 384 * m:384 * m + 384], 1, 0).astype(BF)
        for r in range(2):
            for a in range(NA):
                for t in range(48):
                    z_ref[a, :, 24 * t:24 * t + 24] = y[16 * t:16 * t + 16, C * r + 24 * a:C * r + 24 * a + 24]
            for p in range(NP):
                o_ref[8 * p:8 * p + 8, 2 * m + r, :] = z_ref[:, p, :]


def syn_f(x, pi):
    return whole(syn_f_body, (128, 4, W), x, pi, scratch=[pltpu.VMEM((8, 16, W), BF)], name="syn_f")


def syn_g_body(x_ref, p_ref, o_ref, z_ref):
    for m in range(2):
        y = dot(p_ref[m], x_ref[:, 384 * m:384 * m + 384], 1, 0).astype(BF)
        for r in range(2):
            for k in range(SLOTS):
                z_ref[:, C * k:C * k + C] = y[128 * k:128 * k + 128, C * r:C * r + C]
            o_ref[:, 2 * m + r, :] = z_ref[...]


def syn_g(x, pf):
    return whole(syn_g_body, (128, 4, W), x, pf, scratch=[pltpu.VMEM((128, W), BF)], name="syn_g")


def idft_f_body(y_ref, b_ref, o_ref):
    y = y_ref[...].reshape(512, W)
    o_ref[...] = dot(y[:, :1080], b_ref[...], 0, 0).astype(BF)


def idft_f(y, bdt):
    return whole(idft_f_body, (1080, LON), y, bdt, name="idft_f")


def idft_g_body(y_ref, b_ref, o_ref):
    y = y_ref[...].reshape(512, W)
    z = dot(b_ref[...], y, 1, 0).astype(BF)
    for k in range(SLOTS):
        e = z[:768, C * k:C * k + C].reshape(NA, LP, C)
        o = z[768:, C * k:C * k + C].reshape(NA, LP, C)
        o_ref[:, :, 384 * k:384 * k + 384] = jnp.concatenate([e, o], 2)


def idft_g(y, bp):
    return whole(idft_g_body, (NA, LP, 2304), y, bp, name="idft_g")


def order_tables(table, first):
    part = lax.dynamic_slice(table, (0, first, 0), (LAT, 2, DEG))
    part = part.reshape(NP, ROWS, 2, DEG).transpose(2, 0, 1, 3)
    return jnp.pad(part, ((0, 0), (0, 0), (0, 3), (0, 0)))


def on_device(grid_input, cotangent, forward_legendre, inverse_legendre, filter_weight):
    bdt, bpt, bp = [jnp.asarray(t) for t in tables()]
    both = ("polar", "azimuth")
    first = 2 * lax.axis_index("azimuth")
    wire_a = lax.all_to_all(prep(grid_input), "azimuth", 0, 0)

    wire_g = lax.all_to_all(dft_g(cotangent.reshape(1080, LON), bdt), both, 0, 0)

    pf = order_tables(forward_legendre, first)
    pf = pf.reshape(2, NP, SLOTS, NA, DEG).transpose(0, 2, 1, 3, 4).reshape(2, 768, DEG)
    pi = order_tables(inverse_legendre, first)
    pi = pi.transpose(0, 2, 1, 3).reshape(2, 768, DEG)
    cube = filter_weight.reshape(16, 2, C, C)
    upper = jnp.concatenate([cube[:, 0], cube[:, 1]], axis=2)
    lower = jnp.concatenate([-cube[:, 1], cube[:, 0]], axis=2)
    kernel = jnp.concatenate([upper, lower], axis=1)

    def middle(modes, adjoint):
        modes = lax.all_to_all(modes.reshape(16, 16, 768), "polar", 0, 0)
        modes = mix(modes, kernel, adjoint)
        return lax.all_to_all(modes, "polar", 0, 0).reshape(DEG, 768)

    modes_g = middle(leg_g(wire_g, pi), True)
    wire_f = lax.all_to_all(dft_f(wire_a, bpt), both, 0, 0)
    modes_f = middle(leg_f(wire_f, pf), False)

    back_g = lax.all_to_all(syn_g(modes_g, pf), both, 0, 0)
    back_f = lax.all_to_all(syn_f(modes_f, pi), both, 0, 0)
    wire_e = lax.all_to_all(idft_g(back_g, bp), "azimuth", 0, 0)
    filtered = idft_f(back_f, bdt)
    return filtered.reshape(ROWS, 24, LON), post(wire_e)


def solution(mesh):
    return jax.shard_map(
        on_device,
        mesh=mesh,
        in_specs=(
            P("polar", "azimuth"),
            P("polar", "azimuth", None),
            P(None, "polar", None),
            P(None, "polar", None),
            P("polar", None),
        ),
        out_specs=(P("polar", "azimuth", None), P("polar", "azimuth")),
        check_vma=False,
    )
```

time: 656 us -> 272 us (0.41); the launches traced: 646 us -> 271 us
  local copies, waits for them, and re-layouts: 429 us -> 15.1 us
  waiting for transfers between devices: 20.7 us -> 130 us
  Pallas kernels: 0 us -> 67.1 us
  matrix products: 59 us -> 0 us
  blocking collectives: 40.2 us -> 0 us
  starting transfers between devices: 73.9 us -> 53.5 us
  other arithmetic: 22.4 us -> 4.42 us
    unnamed x45 -> x17, local copies, waits for them, and re-layouts: 207 us -> 1.89 us
    all_to_all x19 -> x0, local copies, waits for them, and re-layouts: 122 us -> none  [the longest x2 32.6 us: degree_rows_local(): lax.all_to_all(grid_rows, 'polar', split_axis=0, concat_axis=1, tiled=True)]
    all_to_all x12 -> x10, waiting for transfers between devices: 20.7 us -> 130 us  [the longest x1 35.5 us: on_device(): wire_e = lax.all_to_all(idft_g(back_g, bp), 'azimuth', 0, 0)]
    pallas_call x0 -> x12, Pallas kernels: none -> 67.1 us  [the longest x10 53.7 us: whole(): pl.pallas_call(body, out_shape=jax.ShapeDtypeStruct(out, BF), scratch_sha...]
    dot_general x10 -> x0, matrix products: 59 us -> none  [the longest x2 15.8 us: degree_sum_local(): jnp.einsum('bamrc,baml->blmrc', split_field, split_table, preferred_eleme...]
    convert_element_type x9 -> x0, local copies, waits for them, and re-layouts: 44.9 us -> none  [the longest x2 16.5 us: degree_rows_local(): grid_rows = jnp.einsum('lmrc,aml->amrc', all_degrees, table, preferred_el...]
    all_to_all x2 -> x0, blocking collectives: 40.2 us -> none  [the longest x1 27.3 us: degree_sum_local(): lax.all_to_all(field, 'polar', split_axis=1, concat_axis=0, tiled=True)]
    reshape x10 -> x1, local copies, waits for them, and re-layouts: 38.4 us -> 4.78 us  [on_device(): cube = filter_weight.reshape(16, 2, C, C)]
  transfers between devices with their start and end apart: 12 -> 10, of which waited for: 2 -> 10; matrix products, arithmetic and copies ran while one was open for 52% -> 7% of each run, Pallas kernels for 0% -> 21%
where the time goes in v1:
time: 272 us; the launch traced here: 271 us
  waiting for transfers between devices  130 us (48%)
  Pallas kernels  67.1 us (25%)
  starting transfers between devices  53.5 us (20%)
  local copies, waits for them, and re-layouts  15.1 us (6%)
  other arithmetic  4.42 us (2%)
    pallas_call x10, Pallas kernels, whole(): pl.pallas_call(body, out_shape=jax.ShapeDtypeStruct(out, BF), scratch_sha...  53.7 us
    all_to_all x1, waiting for transfers between devices, on_device(): wire_e = lax.all_to_all(idft_g(back_g, bp), 'azimuth', 0, 0)  35.5 us
    all_to_all x1, waiting for transfers between devices, on_device(): wire_a = lax.all_to_all(prep(grid_input), 'azimuth', 0, 0)  27.7 us
    all_to_all x1, waiting for transfers between devices, on_device(): back_g = lax.all_to_all(syn_g(modes_g, pf), both, 0, 0)  15.9 us
    all_to_all x1, waiting for transfers between devices, on_device(): back_f = lax.all_to_all(syn_f(modes_f, pi), both, 0, 0)  13.5 us
    all_to_all x1, waiting for transfers between devices, on_device(): lax.all_to_all(dft_g(cotangent.reshape(1080, LON), bdt), both, 0, 0)  13.4 us
    all_to_all x1, starting transfers between devices, on_device(): lax.all_to_all(dft_g(cotangent.reshape(1080, LON), bdt), both, 0, 0)  11.5 us
    all_to_all x2, waiting for transfers between devices, middle(): modes = lax.all_to_all(modes.reshape(16, 16, 768), 'polar', 0, 0)  10.3 us
  transfers between devices with their start and end apart: 10, of which 10 were waited for; matrix products, arithmetic and copies ran while one was open for 7% of the time, Pallas kernels for 21%

profile of v1, /device:TPU:1, one launch (start us, length us, event | category | flops | bytes accessed | tf_op | source)
XLA Modules:
  0.0 270.9 jit_solution(13834396908962546836)
XLA Ops:
  0.6 5.7 %dft_g.1 = bf16[128,4,1152]{2,1,0:T(4,128)(2,1)} custom-call(bf16[1080,1440]{1,0:T(8,128)(2,1)} %bitcast.34, bf16[512,1440]{1,0:T(8,128)(2,1)} %constant.18.clone.b_ref), custom_call_target="tpu_custom_call" | custom-call | tf_op jit(solution)/shard_map/dft_g/pallas_call | solution.py:109
  6.3 11.5 %all-to-all-start.5 = ((bf16[128,4,1152]{2,1,0:T(4,128)(2,1)}), bf16[128,4,1152]{2,1,0:T(4,128)(2,1)S(1)}, u32[]{:S(2)}, u32[]{:S(2)}) async-start(bf16[128,4,1152]{2,1,0:T(4,128)(2,1)} %dft_g.1), calls=%async_computation.5 | async-start | bytes 2359296 | tf_op jit(solution)/shard_map/all_to_all | solution.py:251
  17.8 6.9 %prep.1 = bf16[8,96,2304]{2,1,0:T(8,128)(2,1)} custom-call(bf16[45,34560]{1,0:T(8,128)(2,1)} %x_ref.1), custom_call_target="tpu_custom_call" | custom-call | tf_op jit(solution)/shard_map/prep/pallas_call | solution.py:71
  24.7 13.4 %all-to-all-done.5.r_ref = bf16[128,4,1152]{2,1,0:T(4,128)(2,1)S(1)} async-done(((bf16[128,4,1152]{2,1,0:T(4,128)(2,1)}), bf16[128,4,1152]{2,1,0:T(4,128)(2,1)S(1)}, u32[]{:S(2)}, u32[]{:S(2)}) %all-to-all-start.5) | async-done | bytes 1179680 | tf_op jit(solution)/shard_map/all_to_all | solution.py:251
  42.8 5.1 %constant_dynamic-slice_fusion = (bf16[720,2,256]{2,1,0:T(2,128)(2,1)S(1)}, bf16[720,2,256]{2,1,0:T(2,128)(2,1)}) fusion(bf16[720,16,256]{2,1,0:T(8,128)(2,1)} %param.11, s32[]{:T(128)S(6)} %select_n.4, bf16[720,16,256]{2,1,0:T(8,128)(2,1)} %param.10), kind=kLoop, calls=%fused_computation.5 | loop fusion | bytes 2949124 | tf_op jit(solution)/shard_map/dynamic_slice | solution.py:240
  50.0 6.5 %leg_g.1 = bf16[256,768]{1,0:T(8,128)(2,1)} custom-call(bf16[128,4,1152]{2,1,0:T(4,128)(2,1)} %copy-done.2, bf16[2,768,256]{2,1,0:T(8,128)(2,1)} %bitcast.30), custom_call_target="tpu_custom_call" | custom-call | tf_op jit(solution)/shard_map/leg_g/pallas_call | solution.py:109
  56.5 27.7 %all-to-all-done.r_ref = bf16[8,96,2304]{2,1,0:T(8,128)(2,1)S(1)} async-done(((bf16[8,96,2304]{2,1,0:T(8,128)(2,1)}), bf16[8,96,2304]{2,1,0:T(8,128)(2,1)S(1)}, u32[]{:S(2)}, u32[]{:S(2)}) %all-to-all-start) | async-done | bytes 3538976 | tf_op jit(solution)/shard_map/all_to_all | solution.py:249
  84.3 4.8 %all-to-all-start.6 = ((bf16[16,16,768]{2,1,0:T(8,128)(2,1)}), bf16[16,16,768]{2,1,0:T(8,128)(2,1)}, u32[]{:S(2)}, u32[]{:S(2)}) async-start(bf16[16,16,768]{2,1,0:T(8,128)(2,1)} %bitcast.40), calls=%async_computation.6 | async-start | bytes 786432 | tf_op jit(solution)/shard_map/all_to_all | solution.py:263
  89.1 6.0 %dft_f.1 = bf16[128,4,1152]{2,1,0:T(4,128)(2,1)} custom-call(bf16[8,96,2304]{2,1,0:T(8,128)(2,1)} %copy-done, bf16[512,1536]{1,0:T(8,128)(2,1)} %constant.19.clone.b_ref), custom_call_target="tpu_custom_call" | custom-call | tf_op jit(solution)/shard_map/dft_f/pallas_call | solution.py:109
  95.1 4.0 %all-to-all-done.6.r_ref = bf16[16,16,768]{2,1,0:T(8,128)(2,1)} async-done(((bf16[16,16,768]{2,1,0:T(8,128)(2,1)}), bf16[16,16,768]{2,1,0:T(8,128)(2,1)}, u32[]{:S(2)}, u32[]{:S(2)}) %all-to-all-start.6) | async-done | bytes 393248 | tf_op jit(solution)/shard_map/all_to_all | solution.py:263
  99.1 5.6 %all-to-all-start.1 = ((bf16[128,4,1152]{2,1,0:T(4,128)(2,1)}), bf16[128,4,1152]{2,1,0:T(4,128)(2,1)}, u32[]{:S(2)}, u32[]{:S(2)}) async-start(bf16[128,4,1152]{2,1,0:T(4,128)(2,1)} %dft_f.1), calls=%async_computation.1 | async-start | bytes 2359296 | tf_op jit(solution)/shard_map/all_to_all | solution.py:268
  104.7 4.8 %reshape.44 = bf16[16,2,192,192]{3,2,1,0:T(8,128)(2,1)S(1)} reshape(bf16[16,73728]{1,0:T(8,128)(2,1)} %param.12) | data formatting | bytes 4718592 | tf_op jit(solution)/shard_map/reshape | solution.py:257
  109.9 4.3 %maximum_maximum_fusion.k_ref = bf16[16,384,384]{2,1,0:T(8,128)(2,1)} fusion(bf16[16,192,192]{2,1,0:T(8,128)(2,1)S(1)} %get-tuple-element.3, bf16[16,192,192]{2,1,0:T(8,128)(2,1)S(1)} %fusion, bf16[16,192,192]{2,1,0:T(8,128)(2,1)S(1)} %get-tuple-element.2), kind=kLoop, calls=%fused_computation | loop fusion | flops 18874368 | bytes 8257536 | tf_op jit(solution)/shard_map/concatenate | solution.py:260
  114.2 5.1 %mix_g.1 = bf16[16,16,768]{2,1,0:T(8,128)(2,1)} custom-call(bf16[16,16,768]{2,1,0:T(8,128)(2,1)} %all-to-all-done.6.r_ref, bf16[16,384,384]{2,1,0:T(8,128)(2,1)} %maximum_maximum_fusion.k_ref), custom_call_target="tpu_custom_call" | custom-call | tf_op jit(solution)/shard_map/mix_g/pallas_call | solution.py:109
  119.3 5.6 %all-to-all-done.1.r_ref = bf16[128,4,1152]{2,1,0:T(4,128)(2,1)} async-done(((bf16[128,4,1152]{2,1,0:T(4,128)(2,1)}), bf16[128,4,1152]{2,1,0:T(4,128)(2,1)}, u32[]{:S(2)}, u32[]{:S(2)}) %all-to-all-start.1) | async-done | bytes 1179680 | tf_op jit(solution)/shard_map/all_to_all | solution.py:268
  124.9 4.7 %all-to-all-start.7 = ((bf16[16,16,768]{2,1,0:T(8,128)(2,1)}), bf16[16,16,768]{2,1,0:T(8,128)(2,1)S(1)}, u32[]{:S(2)}, u32[]{:S(2)}) async-start(bf16[16,16,768]{2,1,0:T(8,128)(2,1)} %mix_g.1), calls=%async_computation.7 | async-start | bytes 786432 | tf_op jit(solution)/shard_map/all_to_all | solution.py:265
  130.7 4.9 %leg_f.1 = bf16[256,768]{1,0:T(8,128)(2,1)} custom-call(bf16[128,4,1152]{2,1,0:T(4,128)(2,1)} %all-to-all-done.1.r_ref, bf16[2,768,256]{2,1,0:T(8,128)(2,1)} %bitcast.32), custom_call_target="tpu_custom_call" | custom-call | tf_op jit(solution)/shard_map/leg_f/pallas_call | solution.py:109
  135.6 3.9 %all-to-all-done.7 = bf16[16,16,768]{2,1,0:T(8,128)(2,1)S(1)} async-done(((bf16[16,16,768]{2,1,0:T(8,128)(2,1)}), bf16[16,16,768]{2,1,0:T(8,128)(2,1)S(1)}, u32[]{:S(2)}, u32[]{:S(2)}) %all-to-all-start.7) | async-done | bytes 393248 | tf_op jit(solution)/shard_map/all_to_all | solution.py:265
  139.6 4.5 %all-to-all-start.2 = ((bf16[16,16,768]{2,1,0:T(8,128)(2,1)}), bf16[16,16,768]{2,1,0:T(8,128)(2,1)S(1)}, u32[]{:S(2)}, u32[]{:S(2)}) async-start(bf16[16,16,768]{2,1,0:T(8,128)(2,1)} %bitcast.41), calls=%async_computation.2 | async-start | bytes 786432 | tf_op jit(solution)/shard_map/all_to_all | solution.py:263
  147.8 6.2 %all-to-all-done.2.r_ref = bf16[16,16,768]{2,1,0:T(8,128)(2,1)S(1)} async-done(((bf16[16,16,768]{2,1,0:T(8,128)(2,1)}), bf16[16,16,768]{2,1,0:T(8,128)(2,1)S(1)}, u32[]{:S(2)}, u32[]{:S(2)}) %all-to-all-start.2) | async-done | bytes 393248 | tf_op jit(solution)/shard_map/all_to_all | solution.py:263
  154.0 4.6 %all-to-all-start.8 = ((bf16[128,4,1152]{2,1,0:T(4,128)(2,1)}), bf16[128,4,1152]{2,1,0:T(4,128)(2,1)S(1)}, u32[]{:S(2)}, u32[]{:S(2)}) async-start(bf16[128,4,1152]{2,1,0:T(4,128)(2,1)} %syn_g.1), calls=%async_computation.8 | async-start | bytes 2359296 | tf_op jit(solution)/shard_map/all_to_all | solution.py:271
  158.7 4.5 %mix_f.1 = bf16[16,16,768]{2,1,0:T(8,128)(2,1)} custom-call(bf16[16,16,768]{2,1,0:T(8,128)(2,1)} %copy-done.7, bf16[16,384,384]{2,1,0:T(8,128)(2,1)} %maximum_maximum_fusion.k_ref), custom_call_target="tpu_custom_call" | custom-call | tf_op jit(solution)/shard_map/mix_f/pallas_call | solution.py:109
  163.1 15.9 %all-to-all-done.8.y_ref = bf16[128,4,1152]{2,1,0:T(4,128)(2,1)S(1)} async-done(((bf16[128,4,1152]{2,1,0:T(4,128)(2,1)}), bf16[128,4,1152]{2,1,0:T(4,128)(2,1)S(1)}, u32[]{:S(2)}, u32[]{:S(2)}) %all-to-all-start.8) | async-done | bytes 1179680 | tf_op jit(solution)/shard_map/all_to_all | solution.py:271
  179.1 4.7 %all-to-all-start.3 = ((bf16[16,16,768]{2,1,0:T(8,128)(2,1)}), bf16[16,16,768]{2,1,0:T(8,128)(2,1)S(1)}, u32[]{:S(2)}, u32[]{:S(2)}) async-start(bf16[16,16,768]{2,1,0:T(8,128)(2,1)} %mix_f.1), calls=%async_computation.3 | async-start | bytes 786432 | tf_op jit(solution)/shard_map/all_to_all | solution.py:265
  183.8 5.8 %idft_g.1 = bf16[8,96,2304]{2,1,0:T(8,128)(2,1)} custom-call(bf16[128,4,1152]{2,1,0:T(4,128)(2,1)} %copy-done.3, bf16[1536,512]{1,0:T(8,128)(2,1)} %constant.20.clone.b_ref), custom_call_target="tpu_custom_call" | custom-call | tf_op jit(solution)/shard_map/idft_g/pallas_call | solution.py:109
  189.6 4.2 %all-to-all-done.3 = bf16[16,16,768]{2,1,0:T(8,128)(2,1)S(1)} async-done(((bf16[16,16,768]{2,1,0:T(8,128)(2,1)}), bf16[16,16,768]{2,1,0:T(8,128)(2,1)S(1)}, u32[]{:S(2)}, u32[]{:S(2)}) %all-to-all-start.3) | async-done | bytes 393248 | tf_op jit(solution)/shard_map/all_to_all | solution.py:265
  198.2 6.0 %syn_f.1 = bf16[128,4,1152]{2,1,0:T(4,128)(2,1)} custom-call(bf16[256,768]{1,0:T(8,128)(2,1)} %bitcast.39, bf16[2,768,256]{2,1,0:T(8,128)(2,1)} %bitcast.31), custom_call_target="tpu_custom_call" | custom-call | tf_op jit(solution)/shard_map/syn_f/pallas_call | solution.py:109
  204.2 35.5 %all-to-all-done.9.r_ref = bf16[8,96,2304]{2,1,0:T(8,128)(2,1)S(1)} async-done(((bf16[8,96,2304]{2,1,0:T(8,128)(2,1)}), bf16[8,96,2304]{2,1,0:T(8,128)(2,1)S(1)}, u32[]{:S(2)}, u32[]{:S(2)}) %all-to-all-start.9) | async-done | bytes 3538976 | tf_op jit(solution)/shard_map/all_to_all | solution.py:273
  239.7 5.8 %all-to-all-start.4 = ((bf16[128,4,1152]{2,1,0:T(4,128)(2,1)}), bf16[128,4,1152]{2,1,0:T(4,128)(2,1)}, u32[]{:S(2)}, u32[]{:S(2)}) async-start(bf16[128,4,1152]{2,1,0:T(4,128)(2,1)} %syn_f.1), calls=%async_computation.4 | async-start | bytes 2359296 | tf_op jit(solution)/shard_map/all_to_all | solution.py:272
  245.5 6.5 %post.1 = bf16[45,34560]{1,0:T(8,128)(2,1)} custom-call(bf16[8,96,2304]{2,1,0:T(8,128)(2,1)} %copy-done.1), custom_call_target="tpu_custom_call" | custom-call | tf_op jit(solution)/shard_map/post/pallas_call | solution.py:96
  252.0 13.5 %all-to-all-done.4.y_ref = bf16[128,4,1152]{2,1,0:T(4,128)(2,1)} async-done(((bf16[128,4,1152]{2,1,0:T(4,128)(2,1)}), bf16[128,4,1152]{2,1,0:T(4,128)(2,1)}, u32[]{:S(2)}, u32[]{:S(2)}) %all-to-all-start.4) | async-done | bytes 1179680 | tf_op jit(solution)/shard_map/all_to_all | solution.py:272
  265.5 5.4 %idft_f.1 = bf16[1080,1440]{1,0:T(8,128)(2,1)} custom-call(bf16[128,4,1152]{2,1,0:T(4,128)(2,1)} %all-to-all-done.4.y_ref, bf16[512,1440]{1,0:T(8,128)(2,1)} %constant.18.clone.b_ref), custom_call_target="tpu_custom_call" | custom-call | tf_op jit(solution)/shard_map/idft_f/pallas_call | solution.py:109
  (26 shorter events, 16.4 us)
Async XLA Ops:
  6.3 31.8 %all-to-all-start.5 = ((bf16[128,4,1152]{2,1,0:T(4,128)(2,1)}), bf16[128,4,1152]{2,1,0:T(4,128)(2,1)S(1)}, u32[]{:S(2)}, u32[]{:S(2)}) async-start(bf16[128,4,1152]{2,1,0:T(4,128)(2,1)} %dft_g.1), calls=%async_computation.5 | async-start | bytes 2359296 | tf_op jit(solution)/shard_map/all_to_all | solution.py:251
  38.1 1.0 copy-start.2
  39.1 45.2 %all-to-all-start = ((bf16[8,96,2304]{2,1,0:T(8,128)(2,1)}), bf16[8,96,2304]{2,1,0:T(8,128)(2,1)S(1)}, u32[]{:S(2)}, u32[]{:S(2)}) async-start(bf16[8,96,2304]{2,1,0:T(8,128)(2,1)} %prep.1), calls=%async_computation | async-start | bytes 7077888 | tf_op jit(solution)/shard_map/all_to_all | solution.py:249
  84.3 4.8 %copy-start = (bf16[8,96,2304]{2,1,0:T(8,128)(2,1)}, bf16[8,96,2304]{2,1,0:T(8,128)(2,1)S(1)}, u32[]{:S(2)}) copy-start(bf16[8,96,2304]{2,1,0:T(8,128)(2,1)S(1)} %all-to-all-done.r_ref) | copy-start | bytes 10616836
  84.3 14.9 %all-to-all-start.6 = ((bf16[16,16,768]{2,1,0:T(8,128)(2,1)}), bf16[16,16,768]{2,1,0:T(8,128)(2,1)}, u32[]{:S(2)}, u32[]{:S(2)}) async-start(bf16[16,16,768]{2,1,0:T(8,128)(2,1)} %bitcast.40), calls=%async_computation.6 | async-start | bytes 786432 | tf_op jit(solution)/shard_map/all_to_all | solution.py:263
  99.1 25.7 %all-to-all-start.1 = ((bf16[128,4,1152]{2,1,0:T(4,128)(2,1)}), bf16[128,4,1152]{2,1,0:T(4,128)(2,1)}, u32[]{:S(2)}, u32[]{:S(2)}) async-start(bf16[128,4,1152]{2,1,0:T(4,128)(2,1)} %dft_f.1), calls=%async_computation.1 | async-start | bytes 2359296 | tf_op jit(solution)/shard_map/all_to_all | solution.py:268
  114.2 15.4 %copy-start.4 = (bf16[720,2,256]{2,1,0:T(2,128)(2,1)S(1)}, bf16[720,2,256]{2,1,0:T(2,128)(2,1)}, u32[]{:S(2)}) copy-start(bf16[720,2,256]{2,1,0:T(2,128)(2,1)} %get-tuple-element.5) | copy-start | bytes 2211844
  124.9 14.7 %all-to-all-start.7 = ((bf16[16,16,768]{2,1,0:T(8,128)(2,1)}), bf16[16,16,768]{2,1,0:T(8,128)(2,1)S(1)}, u32[]{:S(2)}, u32[]{:S(2)}) async-start(bf16[16,16,768]{2,1,0:T(8,128)(2,1)} %mix_g.1), calls=%async_computation.7 | async-start | bytes 786432 | tf_op jit(solution)/shard_map/all_to_all | solution.py:265
  139.6 4.5 %copy-start.5 = (bf16[16,16,768]{2,1,0:T(8,128)(2,1)}, bf16[16,16,768]{2,1,0:T(8,128)(2,1)S(1)}, u32[]{:S(2)}) copy-start(bf16[16,16,768]{2,1,0:T(8,128)(2,1)S(1)} %all-to-all-done.7) | copy-start | bytes 1179652
  139.6 14.5 %all-to-all-start.2 = ((bf16[16,16,768]{2,1,0:T(8,128)(2,1)}), bf16[16,16,768]{2,1,0:T(8,128)(2,1)S(1)}, u32[]{:S(2)}, u32[]{:S(2)}) async-start(bf16[16,16,768]{2,1,0:T(8,128)(2,1)} %bitcast.41), calls=%async_computation.2 | async-start | bytes 786432 | tf_op jit(solution)/shard_map/all_to_all | solution.py:263
  154.0 4.6 %copy-start.7 = (bf16[16,16,768]{2,1,0:T(8,128)(2,1)}, bf16[16,16,768]{2,1,0:T(8,128)(2,1)S(1)}, u32[]{:S(2)}) copy-start(bf16[16,16,768]{2,1,0:T(8,128)(2,1)S(1)} %all-to-all-done.2.r_ref) | copy-start | bytes 1179652
  154.0 25.0 %all-to-all-start.8 = ((bf16[128,4,1152]{2,1,0:T(4,128)(2,1)}), bf16[128,4,1152]{2,1,0:T(4,128)(2,1)S(1)}, u32[]{:S(2)}, u32[]{:S(2)}) async-start(bf16[128,4,1152]{2,1,0:T(4,128)(2,1)} %syn_g.1), calls=%async_computation.8 | async-start | bytes 2359296 | tf_op jit(solution)/shard_map/all_to_all | solution.py:271
  179.1 4.7 %copy-start.3 = (bf16[128,4,1152]{2,1,0:T(4,128)(2,1)}, bf16[128,4,1152]{2,1,0:T(4,128)(2,1)S(1)}, u32[]{:S(2)}) copy-start(bf16[128,4,1152]{2,1,0:T(4,128)(2,1)S(1)} %all-to-all-done.8.y_ref) | copy-start | bytes 3538948
  179.1 14.7 %all-to-all-start.3 = ((bf16[16,16,768]{2,1,0:T(8,128)(2,1)}), bf16[16,16,768]{2,1,0:T(8,128)(2,1)S(1)}, u32[]{:S(2)}, u32[]{:S(2)}) async-start(bf16[16,16,768]{2,1,0:T(8,128)(2,1)} %mix_f.1), calls=%async_computation.3 | async-start | bytes 786432 | tf_op jit(solution)/shard_map/all_to_all | solution.py:265
  193.7 0.7 copy-start.6
  194.5 45.2 %all-to-all-start.9 = ((bf16[8,96,2304]{2,1,0:T(8,128)(2,1)}), bf16[8,96,2304]{2,1,0:T(8,128)(2,1)S(1)}, u32[]{:S(2)}, u32[]{:S(2)}) async-start(bf16[8,96,2304]{2,1,0:T(8,128)(2,1)} %idft_g.1), calls=%async_computation.9 | async-start | bytes 7077888 | tf_op jit(solution)/shard_map/all_to_all | solution.py:273
  239.7 5.8 %copy-start.1 = (bf16[8,96,2304]{2,1,0:T(8,128)(2,1)}, bf16[8,96,2304]{2,1,0:T(8,128)(2,1)S(1)}, u32[]{:S(2)}) copy-start(bf16[8,96,2304]{2,1,0:T(8,128)(2,1)S(1)} %all-to-all-done.9.r_ref) | copy-start | bytes 10616836
  239.7 25.8 %all-to-all-start.4 = ((bf16[128,4,1152]{2,1,0:T(4,128)(2,1)}), bf16[128,4,1152]{2,1,0:T(4,128)(2,1)}, u32[]{:S(2)}, u32[]{:S(2)}) async-start(bf16[128,4,1152]{2,1,0:T(4,128)(2,1)} %syn_f.1), calls=%async_computation.4 | async-start | bytes 2359296 | tf_op jit(solution)/shard_map/all_to_all | solution.py:272

commit v2 on v1

v2 whole, which is shorter than its diff:
```python
import functools
import math
import numpy as np
import ml_dtypes
import jax
import jax.numpy as jnp
from jax import lax
from jax.sharding import PartitionSpec as P
from jax.experimental import pallas as pl
from jax.experimental.pallas import tpu as pltpu

LAT = 720
LON = 1440
C = 192
DEG = 256
ORD = 256
NP = 16
NA = 8
ROWS = 45
SLOTS = 6
PAIRS = 90
LP = 96
W = 1152
F32 = jnp.float32
BF = jnp.bfloat16


def params():
    return pltpu.CompilerParams(vmem_limit_bytes=24 << 20)


def dot(a, b, ca, cb):
    return lax.dot_general(a, b, (((ca,), (cb,)), ((), ())), preferred_element_type=F32)


def tables():
    lon = np.arange(LON)[:, None]
    m = np.arange(ORD)[None, :]
    ang = ((lon * m) % LON) * (2.0 * math.pi / LON)
    fac = 1.0 / math.sqrt(LON)
    st = np.stack([np.cos(ang) * fac, -np.sin(ang) * fac], axis=-1).astype(np.float32)
    dbl = np.where(np.arange(ORD) == 0, 1.0, 2.0).astype(np.float32)[None, :, None]
    plain = st.reshape(LON, 2 * ORD).astype(ml_dtypes.bfloat16)
    doubled = (st * dbl).reshape(LON, 2 * ORD).astype(ml_dtypes.bfloat16)
    p4 = plain.reshape(NA, PAIRS, 2, 2 * ORD).transpose(2, 0, 1, 3)
    pp = np.zeros((2, NA, LP, 2 * ORD), ml_dtypes.bfloat16)
    pp[:, :, :PAIRS] = p4
    pp = pp.reshape(2 * NA * LP, 2 * ORD)
    return np.ascontiguousarray(doubled.T), np.ascontiguousarray(pp.T), pp


SMEM = pl.BlockSpec(memory_space=pltpu.SMEM)
VMEM = pl.BlockSpec(memory_space=pltpu.VMEM)


def near(x):
    return pltpu.with_memory_space_constraint(x, pltpu.VMEM)


def prep_body(x_ref, o_ref, s_ref):
    step = pl.program_id(0)
    lane = lax.broadcasted_iota(jnp.int32, (8, 6144), 1) + step * 6144
    good = lane < PAIRS * 384
    for k in range(SLOTS):
        if k < 5:
            v = x_ref[8 * k:8 * k + 8, :].astype(F32)
        else:
            v = jnp.concatenate([x_ref[40:45, :].astype(F32), jnp.zeros((3, 6144), F32)], 0)
        v = jnp.where(good, v, 0.0)
        for lp in range(16):
            for t in range(3):
                s_ref[3 * k + t, pl.ds(lp, 8, stride=17), :] = v[:, (3 * lp + t) * 128:(3 * lp + t + 1) * 128]
    rows = pl.ds(pl.multiple_of(16 * step, 16), 16)
    for a in range(NA):
        for q in range(18):
            o_ref[a, rows, q * 128:(q + 1) * 128] = s_ref[q, 17 * a:17 * a + 16, :].astype(BF)


def prep(x):
    return pl.pallas_call(
        prep_body,
        grid=(6,),
        out_shape=pltpu.VMEM((NA, LP, 2304), BF),
        in_specs=[pl.BlockSpec((ROWS, 6144), lambda i: (0, i))],
        out_specs=VMEM,
        scratch_shapes=[pltpu.VMEM((18, 136, 128), F32)],
        compiler_params=params(),
        name="prep",
    )(x)


def post_body(r_ref, o_ref, s_ref):
    rows = pl.ds(pl.multiple_of(16 * pl.program_id(0), 16), 16)
    for a in range(NA):
        for q in range(18):
            s_ref[q, 17 * a:17 * a + 16, :] = r_ref[a, rows, q * 128:(q + 1) * 128].astype(F32)
    for k in range(SLOTS):
        for lp in range(16):
            for t in range(3):
                v = s_ref[3 * k + t, pl.ds(lp, 8, stride=17), :].astype(BF)
                n = 8 if k < 5 else 5
                o_ref[8 * k:8 * k + n, (3 * lp + t) * 128:(3 * lp + t + 1) * 128] = v[:n]


def post(r):
    return pl.pallas_call(
        post_body,
        grid=(6,),
        out_shape=jax.ShapeDtypeStruct((ROWS, LON // NA * C), BF),
        in_specs=[VMEM],
        out_specs=pl.BlockSpec((ROWS, 6144), lambda i: (0, i)),
        scratch_shapes=[pltpu.VMEM((18, 136, 128), F32)],
        compiler_params=params(),
        name="post",
    )(near(r))


def whole(body, out, *args, scratch=(), name=None, far=False):
    return pl.pallas_call(
        body,
        in_specs=[VMEM] * len(args),
        out_specs=VMEM,
        out_shape=jax.ShapeDtypeStruct(out, BF) if far else pltpu.VMEM(out, BF),
        scratch_shapes=list(scratch),
        compiler_params=params(),
        name=name,
    )(*[near(a) for a in args])


def dft_f_body(r_ref, b_ref, g_ref, o_ref, x_ref):
    for k in range(SLOTS):
        v = r_ref[:, :, 384 * k:384 * k + 384].reshape(NA * LP, 384)
        x_ref[0:768, C * k:C * k + C] = v[:, :C]
        x_ref[768:1536, C * k:C * k + C] = v[:, C:]
    o_ref[:, 4:, :] = g_ref[...]
    y = dot(b_ref[...], x_ref[...], 1, 0).astype(BF)
    o_ref[:, :4, :] = y.reshape(128, 4, W)


def dft_f(r, bpt, wire_g):
    return whole(dft_f_body, (128, 8, W), r, bpt, wire_g, scratch=[pltpu.VMEM((1536, W), BF)], name="dft_f")


def dft_g_body(x_ref, b_ref, o_ref):
    y = dot(b_ref[...], x_ref[...], 1, 1).astype(BF)
    y = jnp.concatenate([y, jnp.zeros((512, W - 1080), BF)], 1)
    o_ref[...] = y.reshape(128, 4, W)


def dft_g(x, bdt):
    return whole(dft_g_body, (128, 4, W), x, bdt, name="dft_g")


def leg_body(r_ref, pf_ref, pi_ref, o_ref, s_ref, t_ref):
    for m in range(2):
        for r in range(2):
            v = r_ref[:, 2 * m + r, :]
            for k in range(SLOTS):
                s_ref[m, 128 * k:128 * k + 128, C * r:C * r + C] = v[:, C * k:C * k + C]
            v = r_ref[:, 4 + 2 * m + r, :].astype(F32).reshape(NP, NA, W)
            for a in range(NA):
                va = v[:, a, :].astype(BF)
                for t in range(48):
                    t_ref[m, 16 * t:16 * t + 16, C * r + 24 * a:C * r + 24 * a + 24] = va[:, 24 * t:24 * t + 24]
        o_ref[:, 384 * m:384 * m + 384] = dot(pf_ref[m], s_ref[m], 0, 0).astype(BF)
        o_ref[:, 768 + 384 * m:768 + 384 * m + 384] = dot(pi_ref[m], t_ref[m], 0, 0).astype(BF)


def leg(r, pf, pi):
    return whole(leg_body, (DEG, 1536), r, pf, pi, scratch=[pltpu.VMEM((2, 768, 384), BF)] * 2, name="leg")


def mix_body(r_ref, k_ref, o_ref, s_ref):
    i = lax.broadcasted_iota(jnp.int32, (256, 256), 0)
    j = lax.broadcasted_iota(jnp.int32, (256, 256), 1)
    perm = ((i // 16 == j % 16) & (i % 16 == j // 16)).astype(F32).astype(BF)
    x = dot(perm, r_ref[...].reshape(256, 1536), 1, 0).astype(BF)
    for l in range(16):
        for side in range(2):
            v = x[16 * l:16 * l + 16, 768 * side:768 * side + 768]
            v = jnp.concatenate([v[:, :384], v[:, 384:]], 0)
            y = dot(v, k_ref[l], 1, side).astype(BF)
            s_ref[16 * l:16 * l + 16, 768 * side:768 * side + 384] = y[:16]
            s_ref[16 * l:16 * l + 16, 768 * side + 384:768 * side + 768] = y[16:]
    o_ref[...] = dot(perm, s_ref[...], 1, 0).astype(BF).reshape(16, 16, 1536)


def mix(r, k):
    return whole(mix_body, (16, 16, 1536), r, k, scratch=[pltpu.VMEM((256, 1536), BF)], name="mix")


def syn_body(x_ref, pf_ref, pi_ref, o_ref, z_ref, y_ref):
    for m in range(2):
        y = dot(pi_ref[m], x_ref[:, 384 * m:384 * m + 384], 1, 0).astype(BF)
        for r in range(2):
            for a in range(NA):
                for t in range(48):
                    z_ref[a, :, 24 * t:24 * t + 24] = y[16 * t:16 * t + 16, C * r + 24 * a:C * r + 24 * a + 24]
            for p in range(NP):
                o_ref[8 * p:8 * p + 8, 2 * m + r, :] = z_ref[:, p, :]
        y = dot(pf_ref[m], x_ref[:, 768 + 384 * m:768 + 384 * m + 384], 1, 0).astype(BF)
        for r in range(2):
            for k in range(SLOTS):
                y_ref[:, C * k:C * k + C] = y[128 * k:128 * k + 128, C * r:C * r + C]
            o_ref[:, 4 + 2 * m + r, :] = y_ref[...]


def syn(x, pf, pi):
    return whole(syn_body, (128, 8, W), x, pf, pi, scratch=[pltpu.VMEM((8, 16, W), BF), pltpu.VMEM((128, W), BF)], name="syn")


def idft_f_body(y_ref, b_ref, o_ref):
    y = y_ref[:, :4, :].reshape(512, W)
    o_ref[...] = dot(y[:, :1080], b_ref[...], 0, 0).astype(BF)


def idft_f(y, bdt):
    return whole(idft_f_body, (1080, LON), y, bdt, name="idft_f", far=True)


def idft_g_body(y_ref, b_ref, o_ref):
    y = y_ref[:, 4:, :].reshape(512, W)
    z = dot(b_ref[...], y, 1, 0).astype(BF)
    for k in range(SLOTS):
        e = z[:768, C * k:C * k + C].reshape(NA, LP, C)
        o = z[768:, C * k:C * k + C].reshape(NA, LP, C)
        o_ref[:, :, 384 * k:384 * k + 384] = jnp.concatenate([e, o], 2)


def idft_g(y, bp):
    return whole(idft_g_body, (NA, LP, 2304), y, bp, name="idft_g")


def order_tables(table, first):
    part = lax.dynamic_slice(table, (0, first, 0), (LAT, 2, DEG))
    part = part.reshape(NP, ROWS, 2, DEG).transpose(2, 0, 1, 3)
    return jnp.pad(part, ((0, 0), (0, 0), (0, 3), (0, 0)))


def fence(*values):
    return lax.optimization_barrier(values)


def on_device(grid_input, cotangent, forward_legendre, inverse_legendre, filter_weight):
    bdt, bpt, bp = [jnp.asarray(t) for t in tables()]
    both = ("polar", "azimuth")
    first = 2 * lax.axis_index("azimuth")

    def over_all(x):
        return lax.all_to_all(x, both, 0, 0)

    def over_polar(x):
        return lax.all_to_all(x, "polar", 0, 0)

    def over_azimuth(x):
        return lax.all_to_all(x, "azimuth", 0, 0)

    spread = prep(grid_input)
    cot = cotangent.reshape(1080, LON)
    spread, cot = fence(spread, cot)
    got = over_azimuth(spread)
    wire_g = dft_g(cot, bdt)

    pf = order_tables(forward_legendre, first)
    pf = pf.reshape(2, NP, SLOTS, NA, DEG).transpose(0, 2, 1, 3, 4).reshape(2, 768, DEG)
    pi = order_tables(inverse_legendre, first)
    pi = pi.transpose(0, 2, 1, 3).reshape(2, 768, DEG)
    cube = filter_weight.reshape(16, 2, C, C)
    upper = jnp.concatenate([cube[:, 0], cube[:, 1]], axis=2)
    lower = jnp.concatenate([-cube[:, 1], cube[:, 0]], axis=2)
    kernel = jnp.concatenate([upper, lower], axis=1)

    got, wire_g, pf, pi, kernel = fence(got, wire_g, pf, pi, kernel)
    modes = leg(over_all(dft_f(got, bpt, wire_g)), pf, pi)
    modes = over_polar(modes.reshape(16, 16, 1536))
    modes = over_polar(mix(modes, kernel)).reshape(DEG, 1536)
    back = over_all(syn(modes, pf, pi))
    grad = over_azimuth(idft_g(back, bp))
    filtered = idft_f(back, bdt)
    filtered, grad = fence(filtered, grad)
    return filtered.reshape(ROWS, 24, LON), post(grad)


def solution(mesh):
    return jax.shard_map(
        on_device,
        mesh=mesh,
        in_specs=(
            P("polar", "azimuth"),
            P("polar", "azimuth", None),
            P(None, "polar", None),
            P(None, "polar", None),
            P("polar", None),
        ),
        out_specs=(P("polar", "azimuth", None), P("polar", "azimuth")),
        check_vma=False,
    )
```

time: 272 us -> 246 us (0.904)
  blocking collectives: 0 us -> 114 us
  waiting for transfers between devices: 130 us -> 53.6 us
  starting transfers between devices: 53.5 us -> 11.3 us
  Pallas kernels: 67.1 us -> 33.8 us
  local copies, waits for them, and re-layouts: 15.1 us -> 27.4 us
    all_to_all x0 -> x4, blocking collectives: none -> 114 us  [the longest x2 77.3 us: over_all(): return lax.all_to_all(x, both, 0, 0)]
    all_to_all x10 -> x2, waiting for transfers between devices: 130 us -> 53.6 us  [over_azimuth(): return lax.all_to_all(x, 'azimuth', 0, 0)]
    all_to_all x10 -> x2, starting transfers between devices: 53.5 us -> 11.3 us  [over_azimuth(): return lax.all_to_all(x, 'azimuth', 0, 0)]
    pallas_call x11 -> x8, Pallas kernels: 60.6 us -> 28.8 us  [the longest x7 27 us: whole(): pl.pallas_call(body, in_specs=[VMEM] * len(args), out_specs=VMEM, out_sha...]
    unnamed x17 -> x31, local copies, waits for them, and re-layouts: 1.89 us -> 13.6 us
  transfers between devices with their start and end apart: 10 -> 2, of which waited for: 10 -> 2; matrix products, arithmetic and copies ran while one was open for 7% -> 7% of each run, Pallas kernels for 21% -> 2%
where the time goes in v2:
time: 246 us; the launch traced here: 245 us
  blocking collectives  114 us (46%)
  waiting for transfers between devices  53.6 us (22%)
  Pallas kernels  33.8 us (14%)
  local copies, waits for them, and re-layouts  27.4 us (11%)
  starting transfers between devices  11.3 us (5%)
  other arithmetic  4.4 us (2%)
    all_to_all x2, blocking collectives, over_all(): return lax.all_to_all(x, both, 0, 0)  77.3 us
    all_to_all x2, waiting for transfers between devices, over_azimuth(): return lax.all_to_all(x, 'azimuth', 0, 0)  53.6 us
    all_to_all x2, blocking collectives, over_polar(): return lax.all_to_all(x, 'polar', 0, 0)  36.6 us
    pallas_call x7, Pallas kernels, whole(): pl.pallas_call(body, in_specs=[VMEM] * len(args), out_specs=VMEM, out_sha...  27 us
    unnamed x31, local copies, waits for them, and re-layouts  13.6 us
    all_to_all x2, starting transfers between devices, over_azimuth(): return lax.all_to_all(x, 'azimuth', 0, 0)  11.3 us
    reshape x1, local copies, waits for them, and re-layouts, on_device(): cube = filter_weight.reshape(16, 2, C, C)  5.94 us
    pallas_call x1, Pallas kernels, post(): pl.pallas_call(post_body, grid=(6,), out_shape=jax.ShapeDtypeStruct((ROWS...  5.03 us
  transfers between devices with their start and end apart: 2, of which 2 were waited for; matrix products, arithmetic and copies ran while one was open for 7% of the time, Pallas kernels for 2%

profile of v2, /device:TPU:1, one launch (start us, length us, event | category | flops | bytes accessed | tf_op | source)
XLA Modules:
  0.0 245.2 jit_solution(8711107000289904137)
XLA Ops:
  0.6 1.9 copy-done.9
  2.6 1.8 prep.1
  4.4 1.8 copy-done.1
  6.2 6.8 %all-to-all-start = ((bf16[8,96,2304]{2,1,0:T(8,128)(2,1)}), bf16[8,96,2304]{2,1,0:T(8,128)(2,1)S(1)}, u32[]{:S(2)}, u32[]{:S(2)}) async-start(bf16[8,96,2304]{2,1,0:T(8,128)(2,1)} %copy-done.1), calls=%async_computation | async-start | bytes 7077888 | tf_op jit(solution)/shard_map/all_to_all | solution.py:256
  13.0 4.2 %constant_dynamic-slice_fusion = (bf16[720,2,256]{2,1,0:T(2,128)(2,1)S(1)}, bf16[720,2,256]{2,1,0:T(2,128)(2,1)S(1)}) fusion(bf16[720,16,256]{2,1,0:T(8,128)(2,1)} %param.11, s32[]{:T(128)S(6)} %select_n.4, bf16[720,16,256]{2,1,0:T(8,128)(2,1)} %param.10), kind=kLoop, calls=%fused_computation.5 | loop fusion | bytes 2949124 | tf_op jit(solution)/shard_map/dynamic_slice | solution.py:235
  17.4 0.9 copy.16
  18.4 0.8 pad_bitcast_fusion.1
  19.2 1.4 copy.17
  20.6 5.9 %reshape.40 = bf16[16,2,192,192]{3,2,1,0:T(8,128)(2,1)} reshape(bf16[16,73728]{1,0:T(8,128)(2,1)} %param.12) | data formatting | bytes 4718592 | tf_op jit(solution)/shard_map/reshape | solution.py:268
  26.6 1.4 copy-done.4
  28.0 1.9 copy-done.8
  29.9 2.2 dft_g.1.g_ref
  32.6 0.6 copy-done.6
  33.2 4.3 %maximum_maximum_fusion.k_ref = bf16[16,384,384]{2,1,0:T(8,128)(2,1)} fusion(bf16[16,192,192]{2,1,0:T(8,128)(2,1)S(1)} %get-tuple-element.21, bf16[16,192,192]{2,1,0:T(8,128)(2,1)S(1)} %fusion, bf16[16,192,192]{2,1,0:T(8,128)(2,1)S(1)} %get-tuple-element.20), kind=kLoop, calls=%fused_computation | loop fusion | flops 18874368 | bytes 8257536 | tf_op jit(solution)/shard_map/concatenate | solution.py:271
  37.5 17.1 %all-to-all-done.r_ref = bf16[8,96,2304]{2,1,0:T(8,128)(2,1)S(1)} async-done(((bf16[8,96,2304]{2,1,0:T(8,128)(2,1)}), bf16[8,96,2304]{2,1,0:T(8,128)(2,1)S(1)}, u32[]{:S(2)}, u32[]{:S(2)}) %all-to-all-start) | async-done | bytes 3538976 | tf_op jit(solution)/shard_map/all_to_all | solution.py:256
  54.6 1.3 copy-done.7
  55.9 1.4 copy-done.11
  57.3 3.1 %dft_f.1 = bf16[128,8,1152]{2,1,0:T(8,128)(2,1)S(1)} custom-call(bf16[8,96,2304]{2,1,0:T(8,128)(2,1)S(1)} %all-to-all-done.r_ref, bf16[512,1536]{1,0:T(8,128)(2,1)S(1)} %copy-done.11, bf16[128,4,1152]{2,1,0:T(4,128)(2,1)S(1)} %copy-done.7), custom_call_target="tpu_custom_call" | custom-call | tf_op jit(solution)/shard_map/dft_f/pallas_call | solution.py:119
  60.4 40.8 %all_to_all.30.r_ref = bf16[128,8,1152]{2,1,0:T(8,128)(2,1)S(1)} all-to-all(bf16[128,8,1152]{2,1,0:T(8,128)(2,1)S(1)} %dft_f.1), channel_id=1, replica_groups=mesh['polar'=16,'azimuth'=8] {'polar','azimuth'}, dimensions={0} | all-to-all | bytes 4718592 | tf_op jit(solution)/shard_map/all_to_all | solution.py:250
  101.1 7.3 %leg.1 = bf16[256,1536]{1,0:T(8,128)(2,1)S(1)} custom-call(bf16[128,8,1152]{2,1,0:T(8,128)(2,1)S(1)} %all_to_all.30.r_ref, bf16[2,768,256]{2,1,0:T(8,128)(2,1)S(1)} %bitcast.30, bf16[2,768,256]{2,1,0:T(8,128)(2,1)S(1)} %bitcast.32), custom_call_target="tpu_custom_call" | custom-call | tf_op jit(solution)/shard_map/leg/pallas_call | solution.py:119
  108.4 18.8 %all_to_all.31.r_ref = bf16[16,16,1536]{2,1,0:T(8,128)(2,1)S(1)} all-to-all(bf16[16,16,1536]{2,1,0:T(8,128)(2,1)S(1)} %bitcast.36), channel_id=1, replica_groups=mesh['polar'=16,'azimuth'=8] {'polar'}, dimensions={0} | all-to-all | bytes 1572864 | tf_op jit(solution)/shard_map/all_to_all | solution.py:253
  127.2 2.9 %mix.1 = bf16[16,16,1536]{2,1,0:T(8,128)(2,1)S(1)} custom-call(bf16[16,16,1536]{2,1,0:T(8,128)(2,1)S(1)} %all_to_all.31.r_ref, bf16[16,384,384]{2,1,0:T(8,128)(2,1)S(1)} %bitcast.29), custom_call_target="tpu_custom_call" | custom-call | tf_op jit(solution)/shard_map/mix/pallas_call | solution.py:119
  130.1 17.8 %all_to_all.32 = bf16[16,16,1536]{2,1,0:T(8,128)(2,1)S(1)} all-to-all(bf16[16,16,1536]{2,1,0:T(8,128)(2,1)S(1)} %mix.1), channel_id=1, replica_groups=mesh['polar'=16,'azimuth'=8] {'polar'}, dimensions={0} | all-to-all | bytes 1572864 | tf_op jit(solution)/shard_map/all_to_all | solution.py:253
  147.8 5.5 %syn.1 = bf16[128,8,1152]{2,1,0:T(8,128)(2,1)S(1)} custom-call(bf16[256,1536]{1,0:T(8,128)(2,1)S(1)} %bitcast.35, bf16[2,768,256]{2,1,0:T(8,128)(2,1)S(1)} %bitcast.31, bf16[2,768,256]{2,1,0:T(8,128)(2,1)S(1)} %bitcast.33), custom_call_target="tpu_custom_call" | custom-call | tf_op jit(solution)/shard_map/syn/pallas_call | solution.py:119
  153.4 36.6 %all_to_all.33.y_ref = bf16[128,8,1152]{2,1,0:T(8,128)(2,1)S(1)} all-to-all(bf16[128,8,1152]{2,1,0:T(8,128)(2,1)S(1)} %syn.1), channel_id=1, replica_groups=mesh['polar'=16,'azimuth'=8] {'polar','azimuth'}, dimensions={0} | all-to-all | bytes 4718592 | tf_op jit(solution)/shard_map/all_to_all | solution.py:250
  190.0 2.3 idft_g.1
  192.3 1.8 copy-done
  194.1 4.5 %all-to-all-start.5 = ((bf16[8,96,2304]{2,1,0:T(8,128)(2,1)}), bf16[8,96,2304]{2,1,0:T(8,128)(2,1)}, u32[]{:S(2)}, u32[]{:S(2)}) async-start(bf16[8,96,2304]{2,1,0:T(8,128)(2,1)} %copy-done), calls=%async_computation.5 | async-start | bytes 7077888 | tf_op jit(solution)/shard_map/all_to_all | solution.py:256
  198.6 1.4 copy-done.5
  200.0 3.7 %idft_f.1 = bf16[1080,1440]{1,0:T(8,128)(2,1)} custom-call(bf16[128,8,1152]{2,1,0:T(8,128)(2,1)S(1)} %all_to_all.33.y_ref, bf16[512,1440]{1,0:T(8,128)(2,1)S(1)} %copy-done.5), custom_call_target="tpu_custom_call" | custom-call | tf_op jit(solution)/shard_map/idft_f/pallas_call | solution.py:119
  203.7 36.5 %all-to-all-done.5.r_ref = bf16[8,96,2304]{2,1,0:T(8,128)(2,1)} async-done(((bf16[8,96,2304]{2,1,0:T(8,128)(2,1)}), bf16[8,96,2304]{2,1,0:T(8,128)(2,1)}, u32[]{:S(2)}, u32[]{:S(2)}) %all-to-all-start.5) | async-done | bytes 3538976 | tf_op jit(solution)/shard_map/all_to_all | solution.py:256
  240.2 5.0 %post.1 = bf16[45,34560]{1,0:T(8,128)(2,1)} custom-call(bf16[8,96,2304]{2,1,0:T(8,128)(2,1)} %all-to-all-done.5.r_ref), custom_call_target="tpu_custom_call" | custom-call | tf_op jit(solution)/shard_map/post/pallas_call | solution.py:106
  (26 shorter events, 0.7 us)
Async XLA Ops:
  0.6 1.9 copy-start.9
  4.4 1.8 copy-start.1
  6.2 48.4 %all-to-all-start = ((bf16[8,96,2304]{2,1,0:T(8,128)(2,1)}), bf16[8,96,2304]{2,1,0:T(8,128)(2,1)S(1)}, u32[]{:S(2)}, u32[]{:S(2)}) async-start(bf16[8,96,2304]{2,1,0:T(8,128)(2,1)} %copy-done.1), calls=%async_computation | async-start | bytes 7077888 | tf_op jit(solution)/shard_map/all_to_all | solution.py:256
  26.6 1.4 copy-start.4
  28.0 1.9 copy-start.8
  29.9 2.3 copy-start.12
  32.2 1.0 copy-start.6
  54.6 1.3 copy-start.7
  55.9 1.4 copy-start.11
  57.3 43.9 %copy-start.2 = (bf16[2,6,16,8,256]{4,3,2,1,0:T(8,128)(2,1)S(1)}, bf16[2,6,16,8,256]{4,3,2,1,0:T(8,128)(2,1)}, u32[]{:S(2)}) copy-start(bf16[2,6,16,8,256]{4,3,2,1,0:T(8,128)(2,1)} %copy.16) | copy-start | bytes 2359300
  57.3 43.9 %copy-start.3 = (bf16[2,48,16,256]{3,2,1,0:T(8,128)(2,1)S(1)}, bf16[2,48,16,256]{3,2,1,0:T(8,128)(2,1)}, u32[]{:S(2)}) copy-start(bf16[2,48,16,256]{3,2,1,0:T(8,128)(2,1)} %copy.17) | copy-start | bytes 2359300
  57.3 69.9 %slice-start = ((s8[4718592]{0:T(1024)(128)(4,1)}), s8[524288]{0:T(1024)(128)(4,1)S(1)}, s32[]{:S(2)}) async-start(s8[4718592]{0:T(1024)(128)(4,1)} %bitcast.28), calls=%async_computation.6 | async-start | bytes 1048576
  60.4 66.8 %slice-start.1 = ((s8[4718592]{0:T(1024)(128)(4,1)}), s8[4194304]{0:T(1024)(128)(4,1)S(1)}, s32[]{:S(2)}) async-start(s8[4718592]{0:T(1024)(128)(4,1)} %bitcast.28), calls=%async_computation.7 | async-start | bytes 8388608
  153.4 36.6 %copy-start.10 = (bf16[1536,512]{1,0:T(8,128)(2,1)S(1)}, bf16[1536,512]{1,0:T(8,128)(2,1)}, u32[]{:S(2)}) copy-start(bf16[1536,512]{1,0:T(8,128)(2,1)} %constant.20.clone.b_ref) | copy-start | bytes 4718596
  192.3 1.8 copy-start
  194.1 46.1 %all-to-all-start.5 = ((bf16[8,96,2304]{2,1,0:T(8,128)(2,1)}), bf16[8,96,2304]{2,1,0:T(8,128)(2,1)}, u32[]{:S(2)}, u32[]{:S(2)}) async-start(bf16[8,96,2304]{2,1,0:T(8,128)(2,1)} %copy-done), calls=%async_computation.5 | async-start | bytes 7077888 | tf_op jit(solution)/shard_map/all_to_all | solution.py:256
  198.6 1.4 copy-start.5

commit v3 on v2

--- a/solution.py
+++ b/solution.py
@@ -26,7 +26,7 @@
 
 
 def params():
-    return pltpu.CompilerParams(vmem_limit_bytes=24 << 20)
+    return pltpu.CompilerParams(vmem_limit_bytes=16 << 20)
 
 
 def dot(a, b, ca, cb):
@@ -151,22 +151,32 @@
     return whole(dft_g_body, (128, 4, W), x, bdt, name="dft_g")
 
 
+def swap_rows(x, rows, cols):
+    n = rows * cols
+    i = lax.broadcasted_iota(jnp.int32, (n, n), 0)
+    j = lax.broadcasted_iota(jnp.int32, (n, n), 1)
+    perm = ((i // rows == j % cols) & (i % rows == j // cols)).astype(F32).astype(BF)
+    return dot(perm, x, 1, 0).astype(BF)
+
+
 def leg_body(r_ref, pf_ref, pi_ref, o_ref, s_ref, t_ref):
+    for a in range(NA):
+        v = swap_rows(r_ref[:, a, :, :].reshape(128, W), NP, 8)
+        for j in range(4):
+            m, r = j // 2, j % 2
+            for k in range(SLOTS):
+                row = 128 * k + 16 * a
+                s_ref[m, row:row + 16, C * r:C * r + C] = v[16 * j:16 * j + 16, C * k:C * k + C]
+            for t in range(48):
+                lane = C * r + 24 * a
+                t_ref[m, 16 * t:16 * t + 16, lane:lane + 24] = v[64 + 16 * j:80 + 16 * j, 24 * t:24 * t + 24]
     for m in range(2):
-        for r in range(2):
-            v = r_ref[:, 2 * m + r, :]
-            for k in range(SLOTS):
-                s_ref[m, 128 * k:128 * k + 128, C * r:C * r + C] = v[:, C * k:C * k + C]
-            v = r_ref[:, 4 + 2 * m + r, :].astype(F32).reshape(NP, NA, W)
-            for a in range(NA):
-                va = v[:, a, :].astype(BF)
-                for t in range(48):
-                    t_ref[m, 16 * t:16 * t + 16, C * r + 24 * a:C * r + 24 * a + 24] = va[:, 24 * t:24 * t + 24]
         o_ref[:, 384 * m:384 * m + 384] = dot(pf_ref[m], s_ref[m], 0, 0).astype(BF)
         o_ref[:, 768 + 384 * m:768 + 384 * m + 384] = dot(pi_ref[m], t_ref[m], 0, 0).astype(BF)
 
 
 def leg(r, pf, pi):
+    r = r.reshape(NP, NA, 8, W)
     return whole(leg_body, (DEG, 1536), r, pf, pi, scratch=[pltpu.VMEM((2, 768, 384), BF)] * 2, name="leg")
 
 
@@ -189,24 +199,25 @@
     return whole(mix_body, (16, 16, 1536), r, k, scratch=[pltpu.VMEM((256, 1536), BF)], name="mix")
 
 
-def syn_body(x_ref, pf_ref, pi_ref, o_ref, z_ref, y_ref):
+def syn_body(x_ref, pf_ref, pi_ref, o_ref, y_ref, z_ref):
     for m in range(2):
-        y = dot(pi_ref[m], x_ref[:, 384 * m:384 * m + 384], 1, 0).astype(BF)
-        for r in range(2):
-            for a in range(NA):
-                for t in range(48):
-                    z_ref[a, :, 24 * t:24 * t + 24] = y[16 * t:16 * t + 16, C * r + 24 * a:C * r + 24 * a + 24]
-            for p in range(NP):
-                o_ref[8 * p:8 * p + 8, 2 * m + r, :] = z_ref[:, p, :]
-        y = dot(pf_ref[m], x_ref[:, 768 + 384 * m:768 + 384 * m + 384], 1, 0).astype(BF)
-        for r in range(2):
+        y_ref[m] = dot(pi_ref[m], x_ref[:, 384 * m:384 * m + 384], 1, 0).astype(BF)
+        y_ref[2 + m] = dot(pf_ref[m], x_ref[:, 768 + 384 * m:768 + 384 * m + 384], 1, 0).astype(BF)
+    for a in range(NA):
+        for j in range(4):
+            m, r = j // 2, j % 2
+            for t in range(48):
+                lane = C * r + 24 * a
+                z_ref[16 * j:16 * j + 16, 24 * t:24 * t + 24] = y_ref[m, 16 * t:16 * t + 16, lane:lane + 24]
             for k in range(SLOTS):
-                y_ref[:, C * k:C * k + C] = y[128 * k:128 * k + 128, C * r:C * r + C]
-            o_ref[:, 4 + 2 * m + r, :] = y_ref[...]
+                row = 128 * k + 16 * a
+                z_ref[64 + 16 * j:80 + 16 * j, C * k:C * k + C] = y_ref[2 + m, row:row + 16, C * r:C * r + C]
+        o_ref[:, a, :, :] = swap_rows(z_ref[...], 8, NP).reshape(NP, 8, W)
 
 
 def syn(x, pf, pi):
-    return whole(syn_body, (128, 8, W), x, pf, pi, scratch=[pltpu.VMEM((8, 16, W), BF), pltpu.VMEM((128, W), BF)], name="syn")
+    scratch = [pltpu.VMEM((4, 768, 384), BF), pltpu.VMEM((128, W), BF)]
+    return whole(syn_body, (NP, NA, 8, W), x, pf, pi, scratch=scratch, name="syn").reshape(128, 8, W)
 
 
 def idft_f_body(y_ref, b_ref, o_ref):
@@ -233,8 +244,8 @@
 
 def order_tables(table, first):
     part = lax.dynamic_slice(table, (0, first, 0), (LAT, 2, DEG))
-    part = part.reshape(NP, ROWS, 2, DEG).transpose(2, 0, 1, 3)
-    return jnp.pad(part, ((0, 0), (0, 0), (0, 3), (0, 0)))
+    part = part.reshape(NP, ROWS, 2, DEG).transpose(2, 1, 0, 3)
+    return jnp.pad(part, ((0, 0), (0, 3), (0, 0), (0, 0))).reshape(2, 768, DEG)
 
 
 def fence(*values):
@@ -262,15 +273,13 @@
     wire_g = dft_g(cot, bdt)
 
     pf = order_tables(forward_legendre, first)
-    pf = pf.reshape(2, NP, SLOTS, NA, DEG).transpose(0, 2, 1, 3, 4).reshape(2, 768, DEG)
     pi = order_tables(inverse_legendre, first)
-    pi = pi.transpose(0, 2, 1, 3).reshape(2, 768, DEG)
     cube = filter_weight.reshape(16, 2, C, C)
     upper = jnp.concatenate([cube[:, 0], cube[:, 1]], axis=2)
     lower = jnp.concatenate([-cube[:, 1], cube[:, 0]], axis=2)
     kernel = jnp.concatenate([upper, lower], axis=1)
 
-    got, wire_g, pf, pi, kernel = fence(got, wire_g, pf, pi, kernel)
+    got, wire_g, pf, pi, kernel, bpt = fence(got, wire_g, pf, pi, kernel, bpt)
     modes = leg(over_all(dft_f(got, bpt, wire_g)), pf, pi)
     modes = over_polar(modes.reshape(16, 16, 1536))
     modes = over_polar(mix(modes, kernel)).reshape(DEG, 1536)

time: 246 us -> 241 us (0.980)
  Pallas kernels: 33.8 us -> 29.4 us
    pallas_call x7, Pallas kernels: 27 us -> 22.5 us  [whole(): pl.pallas_call(body, in_specs=[VMEM] * len(args), out_specs=VMEM, out_sha...]
    transpose x4 -> x0, local copies, waits for them, and re-layouts: 3.24 us -> none  [the longest x2 2.23 us: on_device(): pi = pi.transpose(0, 2, 1, 3).reshape(2, 768, DEG)]
    unnamed x31 -> x32, local copies, waits for them, and re-layouts: 13.6 us -> 14.2 us
where the time goes in v3:
time: 241 us
  blocking collectives  114 us (47%)
  waiting for transfers between devices  54.4 us (23%)
  Pallas kernels  29.4 us (12%)
  local copies, waits for them, and re-layouts  26.6 us (11%)
  starting transfers between devices  11.3 us (5%)
  other arithmetic  4.42 us (2%)
    all_to_all x2, blocking collectives, over_all(): return lax.all_to_all(x, both, 0, 0)  77.3 us
    all_to_all x2, waiting for transfers between devices, over_azimuth(): return lax.all_to_all(x, 'azimuth', 0, 0)  54.4 us
    all_to_all x2, blocking collectives, over_polar(): return lax.all_to_all(x, 'polar', 0, 0)  36.6 us
    pallas_call x7, Pallas kernels, whole(): pl.pallas_call(body, in_specs=[VMEM] * len(args), out_specs=VMEM, out_sha...  22.5 us
    unnamed x32, local copies, waits for them, and re-layouts  14.2 us
    all_to_all x2, starting transfers between devices, over_azimuth(): return lax.all_to_all(x, 'azimuth', 0, 0)  11.3 us
    reshape x1, local copies, waits for them, and re-layouts, on_device(): cube = filter_weight.reshape(16, 2, C, C)  5.94 us
    pallas_call x1, Pallas kernels, post(): pl.pallas_call(post_body, grid=(6,), out_shape=jax.ShapeDtypeStruct((ROWS...  5.03 us
  transfers between devices with their start and end apart: 2, of which 2 were waited for; matrix products, arithmetic and copies ran while one was open for 7% of the time, Pallas kernels for 2%

profile of v3, /device:TPU:1, one launch (start us, length us, event | category | flops | bytes accessed | tf_op | source)
XLA Modules:
  0.0 240.8 jit_solution(568611361002201296)
XLA Ops:
  0.6 1.9 copy-done.9
  2.6 1.8 prep.1
  4.4 1.8 copy-done.1
  6.2 6.8 %all-to-all-start = ((bf16[8,96,2304]{2,1,0:T(8,128)(2,1)}), bf16[8,96,2304]{2,1,0:T(8,128)(2,1)S(1)}, u32[]{:S(2)}, u32[]{:S(2)}) async-start(bf16[8,96,2304]{2,1,0:T(8,128)(2,1)} %copy-done.1), calls=%async_computation | async-start | bytes 7077888 | tf_op jit(solution)/shard_map/all_to_all | solution.py:267
  13.0 4.2 %constant_dynamic-slice_fusion = (bf16[720,2,256]{2,1,0:T(2,128)(2,1)S(1)}, bf16[720,2,256]{2,1,0:T(2,128)(2,1)S(1)}) fusion(bf16[720,16,256]{2,1,0:T(8,128)(2,1)} %param.11, s32[]{:T(128)S(6)} %select_n.4, bf16[720,16,256]{2,1,0:T(8,128)(2,1)} %param.10), kind=kLoop, calls=%fused_computation.3 | loop fusion | bytes 2949124 | tf_op jit(solution)/shard_map/dynamic_slice | solution.py:246
  17.5 1.0 pad.7.clone
  18.5 0.9 pad.8.clone
  19.4 5.9 %reshape.42 = bf16[16,2,192,192]{3,2,1,0:T(8,128)(2,1)} reshape(bf16[16,73728]{1,0:T(8,128)(2,1)} %param.12) | data formatting | bytes 4718592 | tf_op jit(solution)/shard_map/reshape | solution.py:277
  25.4 1.4 copy-done.4
  26.8 1.9 copy-done.8
  28.7 2.2 dft_g.1.g_ref
  31.0 1.0 copy-done.6
  32.1 0.3 slice_bitcast_fusion
  32.4 4.3 %maximum_maximum_fusion.k_ref = bf16[16,384,384]{2,1,0:T(8,128)(2,1)} fusion(bf16[16,192,192]{2,1,0:T(8,128)(2,1)S(1)} %get-tuple-element.23, bf16[16,192,192]{2,1,0:T(8,128)(2,1)S(1)} %fusion, bf16[16,192,192]{2,1,0:T(8,128)(2,1)S(1)} %get-tuple-element.22), kind=kLoop, calls=%fused_computation | loop fusion | flops 18874368 | bytes 8257536 | tf_op jit(solution)/shard_map/concatenate | solution.py:280
  36.7 17.9 %all-to-all-done.r_ref = bf16[8,96,2304]{2,1,0:T(8,128)(2,1)S(1)} async-done(((bf16[8,96,2304]{2,1,0:T(8,128)(2,1)}), bf16[8,96,2304]{2,1,0:T(8,128)(2,1)S(1)}, u32[]{:S(2)}, u32[]{:S(2)}) %all-to-all-start) | async-done | bytes 3538976 | tf_op jit(solution)/shard_map/all_to_all | solution.py:267
  54.6 1.3 copy-done.7
  55.9 1.4 copy-done.11
  57.3 3.1 %dft_f.1 = bf16[128,8,1152]{2,1,0:T(8,128)(2,1)S(1)} custom-call(bf16[8,96,2304]{2,1,0:T(8,128)(2,1)S(1)} %all-to-all-done.r_ref, bf16[512,1536]{1,0:T(8,128)(2,1)S(1)} %copy-done.11, bf16[128,4,1152]{2,1,0:T(4,128)(2,1)S(1)} %copy-done.7), custom_call_target="tpu_custom_call" | custom-call | tf_op jit(solution)/shard_map/dft_f/pallas_call | solution.py:119
  60.4 40.8 %all_to_all.30 = bf16[128,8,1152]{2,1,0:T(8,128)(2,1)S(1)} all-to-all(bf16[128,8,1152]{2,1,0:T(8,128)(2,1)S(1)} %dft_f.1), channel_id=1, replica_groups=mesh['polar'=16,'azimuth'=8] {'polar','azimuth'}, dimensions={0} | all-to-all | bytes 4718592 | tf_op jit(solution)/shard_map/all_to_all | solution.py:261
  101.1 4.1 %leg.1 = bf16[256,1536]{1,0:T(8,128)(2,1)S(1)} custom-call(bf16[16,8,8,1152]{3,2,1,0:T(8,128)(2,1)S(1)} %bitcast.27, bf16[2,768,256]{2,1,0:T(8,128)(2,1)S(1)} %bitcast.28, bf16[2,768,256]{2,1,0:T(8,128)(2,1)S(1)} %bitcast.30), custom_call_target="tpu_custom_call" | custom-call | tf_op jit(solution)/shard_map/leg/pallas_call | solution.py:119
  105.3 18.8 %all_to_all.31.r_ref = bf16[16,16,1536]{2,1,0:T(8,128)(2,1)S(1)} all-to-all(bf16[16,16,1536]{2,1,0:T(8,128)(2,1)S(1)} %bitcast.34), channel_id=1, replica_groups=mesh['polar'=16,'azimuth'=8] {'polar'}, dimensions={0} | all-to-all | bytes 1572864 | tf_op jit(solution)/shard_map/all_to_all | solution.py:264
  124.1 2.9 %mix.1 = bf16[16,16,1536]{2,1,0:T(8,128)(2,1)S(1)} custom-call(bf16[16,16,1536]{2,1,0:T(8,128)(2,1)S(1)} %all_to_all.31.r_ref, bf16[16,384,384]{2,1,0:T(8,128)(2,1)S(1)} %bitcast.25), custom_call_target="tpu_custom_call" | custom-call | tf_op jit(solution)/shard_map/mix/pallas_call | solution.py:119
  127.0 17.8 %all_to_all.32 = bf16[16,16,1536]{2,1,0:T(8,128)(2,1)S(1)} all-to-all(bf16[16,16,1536]{2,1,0:T(8,128)(2,1)S(1)} %mix.1), channel_id=1, replica_groups=mesh['polar'=16,'azimuth'=8] {'polar'}, dimensions={0} | all-to-all | bytes 1572864 | tf_op jit(solution)/shard_map/all_to_all | solution.py:264
  144.7 4.2 %syn.1 = bf16[16,8,8,1152]{3,2,1,0:T(8,128)(2,1)S(1)} custom-call(bf16[256,1536]{1,0:T(8,128)(2,1)S(1)} %bitcast.33, bf16[2,768,256]{2,1,0:T(8,128)(2,1)S(1)} %bitcast.29, bf16[2,768,256]{2,1,0:T(8,128)(2,1)S(1)} %bitcast.31), custom_call_target="tpu_custom_call" | custom-call | tf_op jit(solution)/shard_map/syn/pallas_call | solution.py:119
  149.0 36.6 %all_to_all.33.y_ref = bf16[128,8,1152]{2,1,0:T(8,128)(2,1)S(1)} all-to-all(bf16[128,8,1152]{2,1,0:T(8,128)(2,1)S(1)} %bitcast.26), channel_id=1, replica_groups=mesh['polar'=16,'azimuth'=8] {'polar','azimuth'}, dimensions={0} | all-to-all | bytes 4718592 | tf_op jit(solution)/shard_map/all_to_all | solution.py:261
  185.5 2.3 idft_g.1
  187.9 1.8 copy-done
  189.7 4.5 %all-to-all-start.5 = ((bf16[8,96,2304]{2,1,0:T(8,128)(2,1)}), bf16[8,96,2304]{2,1,0:T(8,128)(2,1)}, u32[]{:S(2)}, u32[]{:S(2)}) async-start(bf16[8,96,2304]{2,1,0:T(8,128)(2,1)} %copy-done), calls=%async_computation.5 | async-start | bytes 7077888 | tf_op jit(solution)/shard_map/all_to_all | solution.py:267
  194.2 1.4 copy-done.5
  195.6 3.7 %idft_f.1 = bf16[1080,1440]{1,0:T(8,128)(2,1)} custom-call(bf16[128,8,1152]{2,1,0:T(8,128)(2,1)S(1)} %all_to_all.33.y_ref, bf16[512,1440]{1,0:T(8,128)(2,1)S(1)} %copy-done.5), custom_call_target="tpu_custom_call" | custom-call | tf_op jit(solution)/shard_map/idft_f/pallas_call | solution.py:119
  199.2 36.5 %all-to-all-done.5.r_ref = bf16[8,96,2304]{2,1,0:T(8,128)(2,1)} async-done(((bf16[8,96,2304]{2,1,0:T(8,128)(2,1)}), bf16[8,96,2304]{2,1,0:T(8,128)(2,1)}, u32[]{:S(2)}, u32[]{:S(2)}) %all-to-all-start.5) | async-done | bytes 3538976 | tf_op jit(solution)/shard_map/all_to_all | solution.py:267
  235.7 5.0 %post.1 = bf16[45,34560]{1,0:T(8,128)(2,1)} custom-call(bf16[8,96,2304]{2,1,0:T(8,128)(2,1)} %all-to-all-done.5.r_ref), custom_call_target="tpu_custom_call" | custom-call | tf_op jit(solution)/shard_map/post/pallas_call | solution.py:106
  (25 shorter events, 0.4 us)
Async XLA Ops:
  0.6 1.9 copy-start.9
  4.4 1.8 copy-start.1
  6.2 48.4 %all-to-all-start = ((bf16[8,96,2304]{2,1,0:T(8,128)(2,1)}), bf16[8,96,2304]{2,1,0:T(8,128)(2,1)S(1)}, u32[]{:S(2)}, u32[]{:S(2)}) async-start(bf16[8,96,2304]{2,1,0:T(8,128)(2,1)} %copy-done.1), calls=%async_computation | async-start | bytes 7077888 | tf_op jit(solution)/shard_map/all_to_all | solution.py:267
  25.4 1.4 copy-start.4
  26.8 1.9 copy-start.8
  28.7 3.2 %copy-start.12 = (bf16[16,2,192,192]{3,2,1,0:T(8,128)(2,1)S(1)}, bf16[16,2,192,192]{3,2,1,0:T(8,128)(2,1)}, u32[]{:S(2)}) copy-start(bf16[16,2,192,192]{3,2,1,0:T(8,128)(2,1)} %reshape.42) | copy-start | bytes 7077892
  31.0 1.0 copy-start.6
  54.6 1.3 copy-start.7
  55.9 1.4 copy-start.11
  57.3 43.9 %copy-start.2 = (bf16[2,48,16,256]{3,2,1,0:T(8,128)(2,1)S(1)}, bf16[2,48,16,256]{3,2,1,0:T(8,128)(2,1)}, u32[]{:S(2)}) copy-start(bf16[2,48,16,256]{3,2,1,0:T(8,128)(2,1)} %pad.7.clone) | copy-start | bytes 2359300
  57.3 43.9 %copy-start.3 = (bf16[2,48,16,256]{3,2,1,0:T(8,128)(2,1)S(1)}, bf16[2,48,16,256]{3,2,1,0:T(8,128)(2,1)}, u32[]{:S(2)}) copy-start(bf16[2,48,16,256]{3,2,1,0:T(8,128)(2,1)} %pad.8.clone) | copy-start | bytes 2359300
  57.3 66.8 %slice-start = ((s8[4718592]{0:T(1024)(128)(4,1)}), s8[524288]{0:T(1024)(128)(4,1)S(1)}, s32[]{:S(2)}) async-start(s8[4718592]{0:T(1024)(128)(4,1)} %bitcast.24), calls=%async_computation.6 | async-start | bytes 1048576
  60.4 63.7 %slice-start.1 = ((s8[4718592]{0:T(1024)(128)(4,1)}), s8[4194304]{0:T(1024)(128)(4,1)S(1)}, s32[]{:S(2)}) async-start(s8[4718592]{0:T(1024)(128)(4,1)} %bitcast.24), calls=%async_computation.7 | async-start | bytes 8388608
  148.9 36.6 %copy-start.10 = (bf16[1536,512]{1,0:T(8,128)(2,1)S(1)}, bf16[1536,512]{1,0:T(8,128)(2,1)}, u32[]{:S(2)}) copy-start(bf16[1536,512]{1,0:T(8,128)(2,1)} %constant.20.clone.b_ref) | copy-start | bytes 4718596
  187.9 1.8 copy-start
  189.7 46.1 %all-to-all-start.5 = ((bf16[8,96,2304]{2,1,0:T(8,128)(2,1)}), bf16[8,96,2304]{2,1,0:T(8,128)(2,1)}, u32[]{:S(2)}, u32[]{:S(2)}) async-start(bf16[8,96,2304]{2,1,0:T(8,128)(2,1)} %copy-done), calls=%async_computation.5 | async-start | bytes 7077888 | tf_op jit(solution)/shard_map/all_to_all | solution.py:267
  194.2 1.4 copy-start.5

commit v4 on v3

--- a/solution.py
+++ b/solution.py
@@ -26,7 +26,7 @@
 
 
 def params():
-    return pltpu.CompilerParams(vmem_limit_bytes=16 << 20)
+    return pltpu.CompilerParams(vmem_limit_bytes=20 << 20)
 
 
 def dot(a, b, ca, cb):
@@ -42,8 +42,8 @@
     dbl = np.where(np.arange(ORD) == 0, 1.0, 2.0).astype(np.float32)[None, :, None]
     plain = st.reshape(LON, 2 * ORD).astype(ml_dtypes.bfloat16)
     doubled = (st * dbl).reshape(LON, 2 * ORD).astype(ml_dtypes.bfloat16)
-    p4 = plain.reshape(NA, PAIRS, 2, 2 * ORD).transpose(2, 0, 1, 3)
-    pp = np.zeros((2, NA, LP, 2 * ORD), ml_dtypes.bfloat16)
+    p4 = plain.reshape(NA, PAIRS, 2, 2 * ORD).transpose(0, 2, 1, 3)
+    pp = np.zeros((NA, 2, LP, 2 * ORD), ml_dtypes.bfloat16)
     pp[:, :, :PAIRS] = p4
     pp = pp.reshape(2 * NA * LP, 2 * ORD)
     return np.ascontiguousarray(doubled.T), np.ascontiguousarray(pp.T), pp
@@ -53,66 +53,109 @@
 VMEM = pl.BlockSpec(memory_space=pltpu.VMEM)
 
 
+ANY = pl.BlockSpec(memory_space=pl.ANY)
+
+
+def away(x):
+    return pltpu.with_memory_space_constraint(x, pltpu.HBM)
+
+
 def near(x):
     return pltpu.with_memory_space_constraint(x, pltpu.VMEM)
 
 
-def prep_body(x_ref, o_ref, s_ref):
-    step = pl.program_id(0)
-    lane = lax.broadcasted_iota(jnp.int32, (8, 6144), 1) + step * 6144
-    good = lane < PAIRS * 384
-    for k in range(SLOTS):
-        if k < 5:
-            v = x_ref[8 * k:8 * k + 8, :].astype(F32)
-        else:
-            v = jnp.concatenate([x_ref[40:45, :].astype(F32), jnp.zeros((3, 6144), F32)], 0)
-        v = jnp.where(good, v, 0.0)
-        for lp in range(16):
-            for t in range(3):
-                s_ref[3 * k + t, pl.ds(lp, 8, stride=17), :] = v[:, (3 * lp + t) * 128:(3 * lp + t + 1) * 128]
-    rows = pl.ds(pl.multiple_of(16 * step, 16), 16)
-    for a in range(NA):
-        for q in range(18):
-            o_ref[a, rows, q * 128:(q + 1) * 128] = s_ref[q, 17 * a:17 * a + 16, :].astype(BF)
+CHUNKS = [(6144 * i, min(6144, PAIRS * 384 - 6144 * i)) for i in range(6)]
+
+
+def prep_body(x_hbm, o_hbm, x_ref, y_ref, s_ref, in_sem, out_sem):
+    loads = []
+    for i, (lane, n) in enumerate(CHUNKS):
+        part = pl.ds(lane, n)
+        loads.append(pltpu.make_async_copy(x_hbm.at[:, part], x_ref.at[:, part], in_sem.at[i]))
+        loads[i].start()
+    stores = []
+    for i, (lane, n) in enumerate(CHUNKS):
+        loads[i].wait()
+        for k in range(SLOTS):
+            if k < 5:
+                v = x_ref[8 * k:8 * k + 8, lane:lane + n].astype(F32)
+            else:
+                v = jnp.concatenate([x_ref[40:45, lane:lane + n].astype(F32), jnp.zeros((3, n), F32)], 0)
+            for lp in range(16):
+                for t in range(3):
+                    at = (3 * lp + t) * 128
+                    w = v[:, at:at + 128] if at < n else jnp.zeros((8, 128), F32)
+                    s_ref[3 * k + t, pl.ds(lp, 8, stride=17), :] = w
+        for a in range(NA):
+            for q in range(18):
+                y_ref[a, 16 * i:16 * i + 16, q * 128:(q + 1) * 128] = s_ref[q, 17 * a:17 * a + 16, :].astype(BF)
+        part = pl.ds(16 * i, 16)
+        stores.append(pltpu.make_async_copy(y_ref.at[:, part, :], o_hbm.at[:, part, :], out_sem.at[i]))
+        stores[i].start()
+    for copy in stores:
+        copy.wait()
 
 
 def prep(x):
     return pl.pallas_call(
         prep_body,
-        grid=(6,),
-        out_shape=pltpu.VMEM((NA, LP, 2304), BF),
-        in_specs=[pl.BlockSpec((ROWS, 6144), lambda i: (0, i))],
-        out_specs=VMEM,
-        scratch_shapes=[pltpu.VMEM((18, 136, 128), F32)],
+        in_specs=[ANY],
+        out_specs=ANY,
+        out_shape=pltpu.HBM((NA, LP, 2304), BF),
+        scratch_shapes=[
+            pltpu.VMEM((ROWS, PAIRS * 384), BF),
+            pltpu.VMEM((NA, LP, 2304), BF),
+            pltpu.VMEM((18, 136, 128), F32),
+            pltpu.SemaphoreType.DMA((6,)),
+            pltpu.SemaphoreType.DMA((6,)),
+        ],
         compiler_params=params(),
         name="prep",
-    )(x)
-
-
-def post_body(r_ref, o_ref, s_ref):
-    rows = pl.ds(pl.multiple_of(16 * pl.program_id(0), 16), 16)
-    for a in range(NA):
-        for q in range(18):
-            s_ref[q, 17 * a:17 * a + 16, :] = r_ref[a, rows, q * 128:(q + 1) * 128].astype(F32)
-    for k in range(SLOTS):
-        for lp in range(16):
-            for t in range(3):
-                v = s_ref[3 * k + t, pl.ds(lp, 8, stride=17), :].astype(BF)
-                n = 8 if k < 5 else 5
-                o_ref[8 * k:8 * k + n, (3 * lp + t) * 128:(3 * lp + t + 1) * 128] = v[:n]
+    )(away(x))
+
+
+def post_body(r_hbm, o_hbm, r_ref, y_ref, s_ref, in_sem, out_sem):
+    loads = []
+    for i in range(6):
+        part = pl.ds(16 * i, 16)
+        loads.append(pltpu.make_async_copy(r_hbm.at[:, part, :], r_ref.at[:, part, :], in_sem.at[i]))
+        loads[i].start()
+    stores = []
+    for i, (lane, n) in enumerate(CHUNKS):
+        loads[i].wait()
+        for a in range(NA):
+            for q in range(18):
+                s_ref[q, 17 * a:17 * a + 16, :] = r_ref[a, 16 * i:16 * i + 16, q * 128:(q + 1) * 128].astype(F32)
+        for k in range(SLOTS):
+            for lp in range(n // 384):
+                for t in range(3):
+                    v = s_ref[3 * k + t, pl.ds(lp, 8, stride=17), :].astype(BF)
+                    c = 8 if k < 5 else 5
+                    at = lane + (3 * lp + t) * 128
+                    y_ref[8 * k:8 * k + c, at:at + 128] = v[:c]
+        part = pl.ds(lane, n)
+        stores.append(pltpu.make_async_copy(y_ref.at[:, part], o_hbm.at[:, part], out_sem.at[i]))
+        stores[i].start()
+    for copy in stores:
+        copy.wait()
 
 
 def post(r):
     return pl.pallas_call(
         post_body,
-        grid=(6,),
-        out_shape=jax.ShapeDtypeStruct((ROWS, LON // NA * C), BF),
-        in_specs=[VMEM],
-        out_specs=pl.BlockSpec((ROWS, 6144), lambda i: (0, i)),
-        scratch_shapes=[pltpu.VMEM((18, 136, 128), F32)],
+        in_specs=[ANY],
+        out_specs=ANY,
+        out_shape=pltpu.HBM((ROWS, PAIRS * 384), BF),
+        scratch_shapes=[
+            pltpu.VMEM((NA, LP, 2304), BF),
+            pltpu.VMEM((ROWS, PAIRS * 384), BF),
+            pltpu.VMEM((18, 136, 128), F32),
+            pltpu.SemaphoreType.DMA((6,)),
+            pltpu.SemaphoreType.DMA((6,)),
+        ],
         compiler_params=params(),
         name="post",
-    )(near(r))
+    )(away(r))
 
 
 def whole(body, out, *args, scratch=(), name=None, far=False):
@@ -127,18 +170,39 @@
     )(*[near(a) for a in args])
 
 
-def dft_f_body(r_ref, b_ref, g_ref, o_ref, x_ref):
-    for k in range(SLOTS):
-        v = r_ref[:, :, 384 * k:384 * k + 384].reshape(NA * LP, 384)
-        x_ref[0:768, C * k:C * k + C] = v[:, :C]
-        x_ref[768:1536, C * k:C * k + C] = v[:, C:]
+def dft_f_body(r_ref, b_hbm, g_hbm, o_ref, x_ref, b_ref, g_ref, sem):
+    load_b = pltpu.make_async_copy(b_hbm, b_ref, sem.at[0])
+    load_g = pltpu.make_async_copy(g_hbm, g_ref, sem.at[1])
+    load_b.start()
+    load_g.start()
+    for blk in range(NA):
+        for k in range(SLOTS):
+            v = r_ref[blk, :, 384 * k:384 * k + 384]
+            row = 2 * LP * blk
+            x_ref[row:row + LP, C * k:C * k + C] = v[:, :C]
+            x_ref[row + LP:row + 2 * LP, C * k:C * k + C] = v[:, C:]
+    load_b.wait()
+    y = dot(b_ref[...], x_ref[...], 1, 0).astype(BF)
+    load_g.wait()
     o_ref[:, 4:, :] = g_ref[...]
-    y = dot(b_ref[...], x_ref[...], 1, 0).astype(BF)
     o_ref[:, :4, :] = y.reshape(128, 4, W)
 
 
 def dft_f(r, bpt, wire_g):
-    return whole(dft_f_body, (128, 8, W), r, bpt, wire_g, scratch=[pltpu.VMEM((1536, W), BF)], name="dft_f")
+    return pl.pallas_call(
+        dft_f_body,
+        in_specs=[VMEM, ANY, ANY],
+        out_specs=VMEM,
+        out_shape=pltpu.VMEM((128, 8, W), BF),
+        scratch_shapes=[
+            pltpu.VMEM((1536, W), BF),
+            pltpu.VMEM((512, 1536), BF),
+            pltpu.VMEM((128, 4, W), BF),
+            pltpu.SemaphoreType.DMA((2,)),
+        ],
+        compiler_params=params(),
+        name="dft_f",
+    )(near(r), away(bpt), away(wire_g))
 
 
 def dft_g_body(x_ref, b_ref, o_ref):
@@ -229,17 +293,34 @@
     return whole(idft_f_body, (1080, LON), y, bdt, name="idft_f", far=True)
 
 
-def idft_g_body(y_ref, b_ref, o_ref):
+def idft_g_body(y_ref, b_ref, o_hbm, o_ref, sem):
     y = y_ref[:, 4:, :].reshape(512, W)
-    z = dot(b_ref[...], y, 1, 0).astype(BF)
-    for k in range(SLOTS):
-        e = z[:768, C * k:C * k + C].reshape(NA, LP, C)
-        o = z[768:, C * k:C * k + C].reshape(NA, LP, C)
-        o_ref[:, :, 384 * k:384 * k + 384] = jnp.concatenate([e, o], 2)
+    stores = []
+    for i in range(4):
+        z = dot(b_ref[4 * LP * i:4 * LP * (i + 1), :], y, 1, 0).astype(BF)
+        for half in range(2):
+            row = 2 * LP * half
+            for k in range(SLOTS):
+                e = z[row:row + LP, C * k:C * k + C]
+                o = z[row + LP:row + 2 * LP, C * k:C * k + C]
+                o_ref[2 * i + half, :, 384 * k:384 * k + 384] = jnp.concatenate([e, o], 1)
+        part = pl.ds(2 * i, 2)
+        stores.append(pltpu.make_async_copy(o_ref.at[part], o_hbm.at[part], sem.at[i]))
+        stores[i].start()
+    for copy in stores:
+        copy.wait()
 
 
 def idft_g(y, bp):
-    return whole(idft_g_body, (NA, LP, 2304), y, bp, name="idft_g")
+    return pl.pallas_call(
+        idft_g_body,
+        in_specs=[VMEM, VMEM],
+        out_specs=ANY,
+        out_shape=pltpu.HBM((NA, LP, 2304), BF),
+        scratch_shapes=[pltpu.VMEM((NA, LP, 2304), BF), pltpu.SemaphoreType.DMA((4,))],
+        compiler_params=params(),
+        name="idft_g",
+    )(near(y), near(bp))
 
 
 def order_tables(table, first):
@@ -279,7 +360,7 @@
     lower = jnp.concatenate([-cube[:, 1], cube[:, 0]], axis=2)
     kernel = jnp.concatenate([upper, lower], axis=1)
 
-    got, wire_g, pf, pi, kernel, bpt = fence(got, wire_g, pf, pi, kernel, bpt)
+    got, wire_g, pf, pi, kernel = fence(got, wire_g, pf, pi, kernel)
     modes = leg(over_all(dft_f(got, bpt, wire_g)), pf, pi)
     modes = over_polar(modes.reshape(16, 16, 1536))
     modes = over_polar(mix(modes, kernel)).reshape(DEG, 1536)

time: 241 us -> 235 us (0.975)
  local copies, waits for them, and re-layouts: 26.6 us -> 18 us
    unnamed x32 -> x22, local copies, waits for them, and re-layouts: 14.2 us -> 5.56 us
    pallas_call x2 -> x4, Pallas kernels: 6.88 us -> 14 us  [the longest x1 4.48 us: dft_f(): pl.pallas_call(dft_f_body, in_specs=[VMEM, ANY, ANY], out_specs=VMEM, out...]
    pallas_call x7 -> x5, Pallas kernels: 22.5 us -> 17.1 us  [whole(): pl.pallas_call(body, in_specs=[VMEM] * len(args), out_specs=VMEM, out_sha...]
  transfers between devices with their start and end apart: 2 -> 2, of which waited for: 2 -> 2; matrix products, arithmetic and copies ran while one was open for 7% -> 7% of each run, Pallas kernels for 2% -> 3%
where the time goes in v4:
time: 235 us
  blocking collectives  114 us (49%)
  waiting for transfers between devices  54.9 us (23%)
  Pallas kernels  31.1 us (13%)
  local copies, waits for them, and re-layouts  18 us (8%)
  starting transfers between devices  11.3 us (5%)
  other arithmetic  4.37 us (2%)
    all_to_all x2, blocking collectives, over_all(): return lax.all_to_all(x, both, 0, 0)  77.3 us
    all_to_all x2, waiting for transfers between devices, over_azimuth(): return lax.all_to_all(x, 'azimuth', 0, 0)  54.9 us
    all_to_all x2, blocking collectives, over_polar(): return lax.all_to_all(x, 'polar', 0, 0)  36.6 us
    pallas_call x5, Pallas kernels, whole(): pl.pallas_call(body, in_specs=[VMEM] * len(args), out_specs=VMEM, out_sha...  17.1 us
    all_to_all x2, starting transfers between devices, over_azimuth(): return lax.all_to_all(x, 'azimuth', 0, 0)  11.3 us
    reshape x1, local copies, waits for them, and re-layouts, on_device(): cube = filter_weight.reshape(16, 2, C, C)  5.94 us
    unnamed x22, local copies, waits for them, and re-layouts  5.56 us
  transfers between devices with their start and end apart: 2, of which 2 were waited for; matrix products, arithmetic and copies ran while one was open for 7% of the time, Pallas kernels for 3%

profile of v4, /device:TPU:1, one launch (start us, length us, event | category | flops | bytes accessed | tf_op | source)
XLA Modules:
  0.0 234.5 jit_solution(958665087811787494)
XLA Ops:
  0.6 3.2 %prep.1 = bf16[8,96,2304]{2,1,0:T(8,128)(2,1)} custom-call(bf16[45,34560]{1,0:T(8,128)(2,1)} %x_hbm.1), custom_call_target="tpu_custom_call" | custom-call | tf_op jit(solution)/shard_map/prep/pallas_call | solution.py:100
  3.8 6.8 %all-to-all-start = ((bf16[8,96,2304]{2,1,0:T(8,128)(2,1)}), bf16[8,96,2304]{2,1,0:T(8,128)(2,1)S(1)}, u32[]{:S(2)}, u32[]{:S(2)}) async-start(bf16[8,96,2304]{2,1,0:T(8,128)(2,1)} %prep.1), calls=%async_computation | async-start | bytes 7077888 | tf_op jit(solution)/shard_map/all_to_all | solution.py:348
  10.6 4.2 %constant_dynamic-slice_fusion = (bf16[720,2,256]{2,1,0:T(2,128)(2,1)S(1)}, bf16[720,2,256]{2,1,0:T(2,128)(2,1)S(1)}) fusion(bf16[720,16,256]{2,1,0:T(8,128)(2,1)} %param.11, s32[]{:T(128)S(6)} %select_n.4, bf16[720,16,256]{2,1,0:T(8,128)(2,1)} %param.10), kind=kLoop, calls=%fused_computation.3 | loop fusion | bytes 2949124 | tf_op jit(solution)/shard_map/dynamic_slice | solution.py:327
  14.9 0.1 copy.17
  15.0 0.1 copy.16
  15.1 0.9 pad.7.clone
  16.0 1.0 pad.8.clone
  17.0 5.9 %reshape.42 = bf16[16,2,192,192]{3,2,1,0:T(8,128)(2,1)} reshape(bf16[16,73728]{1,0:T(8,128)(2,1)} %param.12) | data formatting | bytes 4718592 | tf_op jit(solution)/shard_map/reshape | solution.py:358
  23.0 1.4 copy-done.2
  24.4 1.9 copy-done.5
  26.3 2.2 dft_g.1.g_hbm
  28.6 0.1 fusion
  28.7 0.3 slice_bitcast_fusion
  29.0 0.6 copy-done.4
  29.6 4.3 %maximum_maximum_fusion.k_ref = bf16[16,384,384]{2,1,0:T(8,128)(2,1)} fusion(bf16[16,192,192]{2,1,0:T(8,128)(2,1)S(1)} %get-tuple-element.21, bf16[16,192,192]{2,1,0:T(8,128)(2,1)S(1)} %fusion, bf16[16,192,192]{2,1,0:T(8,128)(2,1)S(1)} %get-tuple-element.20), kind=kLoop, calls=%fused_computation | loop fusion | flops 18874368 | bytes 8257536 | tf_op jit(solution)/shard_map/concatenate | solution.py:361
  33.8 18.4 %all-to-all-done.r_ref = bf16[8,96,2304]{2,1,0:T(8,128)(2,1)S(1)} async-done(((bf16[8,96,2304]{2,1,0:T(8,128)(2,1)}), bf16[8,96,2304]{2,1,0:T(8,128)(2,1)S(1)}, u32[]{:S(2)}, u32[]{:S(2)}) %all-to-all-start) | async-done | bytes 3538976 | tf_op jit(solution)/shard_map/all_to_all | solution.py:348
  52.2 4.5 %dft_f.1 = bf16[128,8,1152]{2,1,0:T(8,128)(2,1)S(1)} custom-call(bf16[8,96,2304]{2,1,0:T(8,128)(2,1)S(1)} %all-to-all-done.r_ref, bf16[512,1536]{1,0:T(8,128)(2,1)} %constant.19.clone.b_hbm, bf16[128,4,1152]{2,1,0:T(4,128)(2,1)} %copy-done.4), custom_call_target="tpu_custom_call" | custom-call | tf_op jit(solution)/shard_map/dft_f/pallas_call | solution.py:192
  56.7 40.8 %all_to_all.30 = bf16[128,8,1152]{2,1,0:T(8,128)(2,1)S(1)} all-to-all(bf16[128,8,1152]{2,1,0:T(8,128)(2,1)S(1)} %dft_f.1), channel_id=1, replica_groups=mesh['polar'=16,'azimuth'=8] {'polar','azimuth'}, dimensions={0} | all-to-all | bytes 4718592 | tf_op jit(solution)/shard_map/all_to_all | solution.py:342
  97.5 4.1 %leg.1 = bf16[256,1536]{1,0:T(8,128)(2,1)S(1)} custom-call(bf16[16,8,8,1152]{3,2,1,0:T(8,128)(2,1)S(1)} %bitcast.27, bf16[2,768,256]{2,1,0:T(8,128)(2,1)S(1)} %bitcast.28, bf16[2,768,256]{2,1,0:T(8,128)(2,1)S(1)} %bitcast.30), custom_call_target="tpu_custom_call" | custom-call | tf_op jit(solution)/shard_map/leg/pallas_call | solution.py:162
  101.6 18.8 %all_to_all.31.r_ref = bf16[16,16,1536]{2,1,0:T(8,128)(2,1)S(1)} all-to-all(bf16[16,16,1536]{2,1,0:T(8,128)(2,1)S(1)} %bitcast.34), channel_id=1, replica_groups=mesh['polar'=16,'azimuth'=8] {'polar'}, dimensions={0} | all-to-all | bytes 1572864 | tf_op jit(solution)/shard_map/all_to_all | solution.py:345
  120.4 2.9 %mix.1 = bf16[16,16,1536]{2,1,0:T(8,128)(2,1)S(1)} custom-call(bf16[16,16,1536]{2,1,0:T(8,128)(2,1)S(1)} %all_to_all.31.r_ref, bf16[16,384,384]{2,1,0:T(8,128)(2,1)S(1)} %bitcast.25), custom_call_target="tpu_custom_call" | custom-call | tf_op jit(solution)/shard_map/mix/pallas_call | solution.py:162
  123.3 17.8 %all_to_all.32 = bf16[16,16,1536]{2,1,0:T(8,128)(2,1)S(1)} all-to-all(bf16[16,16,1536]{2,1,0:T(8,128)(2,1)S(1)} %mix.1), channel_id=1, replica_groups=mesh['polar'=16,'azimuth'=8] {'polar'}, dimensions={0} | all-to-all | bytes 1572864 | tf_op jit(solution)/shard_map/all_to_all | solution.py:345
  141.1 4.2 %syn.1 = bf16[16,8,8,1152]{3,2,1,0:T(8,128)(2,1)S(1)} custom-call(bf16[256,1536]{1,0:T(8,128)(2,1)S(1)} %bitcast.33, bf16[2,768,256]{2,1,0:T(8,128)(2,1)S(1)} %bitcast.29, bf16[2,768,256]{2,1,0:T(8,128)(2,1)S(1)} %bitcast.31), custom_call_target="tpu_custom_call" | custom-call | tf_op jit(solution)/shard_map/syn/pallas_call | solution.py:162
  145.3 0.0 copy-start.6
  145.3 36.6 %all_to_all.33.y_ref = bf16[128,8,1152]{2,1,0:T(8,128)(2,1)S(1)} all-to-all(bf16[128,8,1152]{2,1,0:T(8,128)(2,1)S(1)} %bitcast.26), channel_id=1, replica_groups=mesh['polar'=16,'azimuth'=8] {'polar','azimuth'}, dimensions={0} | all-to-all | bytes 4718592 | tf_op jit(solution)/shard_map/all_to_all | solution.py:342
  181.9 3.3 %idft_g.1 = bf16[8,96,2304]{2,1,0:T(8,128)(2,1)} custom-call(bf16[128,8,1152]{2,1,0:T(8,128)(2,1)S(1)} %all_to_all.33.y_ref, bf16[1536,512]{1,0:T(8,128)(2,1)S(1)} %copy-done.6), custom_call_target="tpu_custom_call" | custom-call | tf_op jit(solution)/shard_map/idft_g/pallas_call | solution.py:315
  185.2 4.5 %all-to-all-start.5 = ((bf16[8,96,2304]{2,1,0:T(8,128)(2,1)}), bf16[8,96,2304]{2,1,0:T(8,128)(2,1)}, u32[]{:S(2)}, u32[]{:S(2)}) async-start(bf16[8,96,2304]{2,1,0:T(8,128)(2,1)} %idft_g.1), calls=%async_computation.5 | async-start | bytes 7077888 | tf_op jit(solution)/shard_map/all_to_all | solution.py:348
  189.7 0.0 copy-start.3
  189.8 1.4 copy-done.3
  191.2 3.7 %idft_f.1 = bf16[1080,1440]{1,0:T(8,128)(2,1)} custom-call(bf16[128,8,1152]{2,1,0:T(8,128)(2,1)S(1)} %all_to_all.33.y_ref, bf16[512,1440]{1,0:T(8,128)(2,1)S(1)} %copy-done.3), custom_call_target="tpu_custom_call" | custom-call | tf_op jit(solution)/shard_map/idft_f/pallas_call | solution.py:162
  194.8 36.5 %all-to-all-done.5.r_hbm = bf16[8,96,2304]{2,1,0:T(8,128)(2,1)} async-done(((bf16[8,96,2304]{2,1,0:T(8,128)(2,1)}), bf16[8,96,2304]{2,1,0:T(8,128)(2,1)}, u32[]{:S(2)}, u32[]{:S(2)}) %all-to-all-start.5) | async-done | bytes 3538976 | tf_op jit(solution)/shard_map/all_to_all | solution.py:348
  231.3 3.0 %post.1 = bf16[45,34560]{1,0:T(8,128)(2,1)} custom-call(bf16[8,96,2304]{2,1,0:T(8,128)(2,1)} %all-to-all-done.5.r_hbm), custom_call_target="tpu_custom_call" | custom-call | tf_op jit(solution)/shard_map/post/pallas_call | solution.py:144
  (15 shorter events, 0.0 us)
Async XLA Ops:
  3.8 48.4 %all-to-all-start = ((bf16[8,96,2304]{2,1,0:T(8,128)(2,1)}), bf16[8,96,2304]{2,1,0:T(8,128)(2,1)S(1)}, u32[]{:S(2)}, u32[]{:S(2)}) async-start(bf16[8,96,2304]{2,1,0:T(8,128)(2,1)} %prep.1), calls=%async_computation | async-start | bytes 7077888 | tf_op jit(solution)/shard_map/all_to_all | solution.py:348
  23.0 1.4 copy-start.2
  24.4 1.9 copy-start.5
  26.3 2.2 copy-start.7
  28.6 1.0 copy-start.4
  52.2 68.2 %slice-start = ((s8[4718592]{0:T(1024)(128)(4,1)}), s8[4194304]{0:T(1024)(128)(4,1)S(1)}, s32[]{:S(2)}) async-start(s8[4718592]{0:T(1024)(128)(4,1)} %bitcast.24), calls=%async_computation.6 | async-start | bytes 8388608
  56.7 40.8 %copy-start = (bf16[2,48,16,256]{3,2,1,0:T(8,128)(2,1)S(1)}, bf16[2,48,16,256]{3,2,1,0:T(8,128)(2,1)}, u32[]{:S(2)}) copy-start(bf16[2,48,16,256]{3,2,1,0:T(8,128)(2,1)} %pad.7.clone) | copy-start | bytes 2359300
  56.7 40.8 %copy-start.1 = (bf16[2,48,16,256]{3,2,1,0:T(8,128)(2,1)S(1)}, bf16[2,48,16,256]{3,2,1,0:T(8,128)(2,1)}, u32[]{:S(2)}) copy-start(bf16[2,48,16,256]{3,2,1,0:T(8,128)(2,1)} %pad.8.clone) | copy-start | bytes 2359300
  56.7 63.7 %slice-start.1 = ((s8[4718592]{0:T(1024)(128)(4,1)}), s8[524288]{0:T(1024)(128)(4,1)S(1)}, s32[]{:S(2)}) async-start(s8[4718592]{0:T(1024)(128)(4,1)} %bitcast.24), calls=%async_computation.7 | async-start | bytes 1048576
  145.3 36.6 %copy-start.6 = (bf16[1536,512]{1,0:T(8,128)(2,1)S(1)}, bf16[1536,512]{1,0:T(8,128)(2,1)}, u32[]{:S(2)}) copy-start(bf16[1536,512]{1,0:T(8,128)(2,1)} %constant.20.clone.b_ref) | copy-start | bytes 4718596
  185.2 46.1 %all-to-all-start.5 = ((bf16[8,96,2304]{2,1,0:T(8,128)(2,1)}), bf16[8,96,2304]{2,1,0:T(8,128)(2,1)}, u32[]{:S(2)}, u32[]{:S(2)}) async-start(bf16[8,96,2304]{2,1,0:T(8,128)(2,1)} %idft_g.1), calls=%async_computation.5 | async-start | bytes 7077888 | tf_op jit(solution)/shard_map/all_to_all | solution.py:348
  189.7 1.4 copy-start.3

commit v5 on v4

--- a/solution.py
+++ b/solution.py
@@ -64,98 +64,90 @@
     return pltpu.with_memory_space_constraint(x, pltpu.VMEM)
 
 
-CHUNKS = [(6144 * i, min(6144, PAIRS * 384 - 6144 * i)) for i in range(6)]
+WIRE = 272 * SLOTS
+STRIDE = 273
+
+
+def slot_rows(k):
+    return pl.ds(8 * k, 8 if k < 5 else 5)
 
 
 def prep_body(x_hbm, o_hbm, x_ref, y_ref, s_ref, in_sem, out_sem):
     loads = []
-    for i, (lane, n) in enumerate(CHUNKS):
-        part = pl.ds(lane, n)
-        loads.append(pltpu.make_async_copy(x_hbm.at[:, part], x_ref.at[:, part], in_sem.at[i]))
-        loads[i].start()
+    for k in range(SLOTS):
+        rows = slot_rows(k)
+        loads.append(pltpu.make_async_copy(x_hbm.at[rows, :], x_ref.at[rows, :], in_sem.at[k]))
+        loads[k].start()
     stores = []
-    for i, (lane, n) in enumerate(CHUNKS):
-        loads[i].wait()
-        for k in range(SLOTS):
+    for k in range(SLOTS):
+        loads[k].wait()
+        for g in range(6):
+            lane, n = 5760 * g, 5760
             if k < 5:
                 v = x_ref[8 * k:8 * k + 8, lane:lane + n].astype(F32)
             else:
                 v = jnp.concatenate([x_ref[40:45, lane:lane + n].astype(F32), jnp.zeros((3, n), F32)], 0)
-            for lp in range(16):
+            for i in range(15):
                 for t in range(3):
-                    at = (3 * lp + t) * 128
-                    w = v[:, at:at + 128] if at < n else jnp.zeros((8, 128), F32)
-                    s_ref[3 * k + t, pl.ds(lp, 8, stride=17), :] = w
+                    at = (3 * i + t) * 128
+                    s_ref[pl.ds(90 * t + 15 * g + i, 8, stride=STRIDE), :] = v[:, at:at + 128]
         for a in range(NA):
-            for q in range(18):
-                y_ref[a, 16 * i:16 * i + 16, q * 128:(q + 1) * 128] = s_ref[q, 17 * a:17 * a + 16, :].astype(BF)
-        part = pl.ds(16 * i, 16)
-        stores.append(pltpu.make_async_copy(y_ref.at[:, part, :], o_hbm.at[:, part, :], out_sem.at[i]))
-        stores[i].start()
+            y_ref[a, 272 * k:272 * k + 272, :] = s_ref[STRIDE * a:STRIDE * a + 272, :].astype(BF)
+        part = pl.ds(272 * k, 272)
+        stores.append(pltpu.make_async_copy(y_ref.at[:, part, :], o_hbm.at[:, part, :], out_sem.at[k]))
+        stores[k].start()
     for copy in stores:
         copy.wait()
 
 
-def prep(x):
+def edge(body, out, x, name):
     return pl.pallas_call(
-        prep_body,
+        body,
         in_specs=[ANY],
         out_specs=ANY,
-        out_shape=pltpu.HBM((NA, LP, 2304), BF),
+        out_shape=pltpu.HBM(out, BF),
         scratch_shapes=[
-            pltpu.VMEM((ROWS, PAIRS * 384), BF),
-            pltpu.VMEM((NA, LP, 2304), BF),
-            pltpu.VMEM((18, 136, 128), F32),
-            pltpu.SemaphoreType.DMA((6,)),
-            pltpu.SemaphoreType.DMA((6,)),
+            pltpu.VMEM(x.shape, BF),
+            pltpu.VMEM(out, BF),
+            pltpu.VMEM((STRIDE * NA, 128), F32),
+            pltpu.SemaphoreType.DMA((SLOTS,)),
+            pltpu.SemaphoreType.DMA((SLOTS,)),
         ],
         compiler_params=params(),
-        name="prep",
+        name=name,
     )(away(x))
+
+
+def prep(x):
+    return edge(prep_body, (NA, WIRE, 128), x, "prep")
 
 
 def post_body(r_hbm, o_hbm, r_ref, y_ref, s_ref, in_sem, out_sem):
     loads = []
-    for i in range(6):
-        part = pl.ds(16 * i, 16)
-        loads.append(pltpu.make_async_copy(r_hbm.at[:, part, :], r_ref.at[:, part, :], in_sem.at[i]))
-        loads[i].start()
+    for k in range(SLOTS):
+        part = pl.ds(272 * k, 272)
+        loads.append(pltpu.make_async_copy(r_hbm.at[:, part, :], r_ref.at[:, part, :], in_sem.at[k]))
+        loads[k].start()
     stores = []
-    for i, (lane, n) in enumerate(CHUNKS):
-        loads[i].wait()
+    for k in range(SLOTS):
+        loads[k].wait()
         for a in range(NA):
-            for q in range(18):
-                s_ref[q, 17 * a:17 * a + 16, :] = r_ref[a, 16 * i:16 * i + 16, q * 128:(q + 1) * 128].astype(F32)
-        for k in range(SLOTS):
-            for lp in range(n // 384):
-                for t in range(3):
-                    v = s_ref[3 * k + t, pl.ds(lp, 8, stride=17), :].astype(BF)
-                    c = 8 if k < 5 else 5
-                    at = lane + (3 * lp + t) * 128
-                    y_ref[8 * k:8 * k + c, at:at + 128] = v[:c]
-        part = pl.ds(lane, n)
-        stores.append(pltpu.make_async_copy(y_ref.at[:, part], o_hbm.at[:, part], out_sem.at[i]))
-        stores[i].start()
+            s_ref[STRIDE * a:STRIDE * a + 272, :] = r_ref[a, 272 * k:272 * k + 272, :].astype(F32)
+        c = 8 if k < 5 else 5
+        for lp in range(PAIRS):
+            for t in range(3):
+                v = s_ref[pl.ds(90 * t + lp, 8, stride=STRIDE), :].astype(BF)
+                at = (3 * lp + t) * 128
+                y_ref[8 * k:8 * k + c, at:at + 128] = v[:c]
+        rows = slot_rows(k)
+        stores.append(pltpu.make_async_copy(y_ref.at[rows, :], o_hbm.at[rows, :], out_sem.at[k]))
+        stores[k].start()
     for copy in stores:
         copy.wait()
 
 
 def post(r):
-    return pl.pallas_call(
-        post_body,
-        in_specs=[ANY],
-        out_specs=ANY,
-        out_shape=pltpu.HBM((ROWS, PAIRS * 384), BF),
-        scratch_shapes=[
-            pltpu.VMEM((NA, LP, 2304), BF),
-            pltpu.VMEM((ROWS, PAIRS * 384), BF),
-            pltpu.VMEM((18, 136, 128), F32),
-            pltpu.SemaphoreType.DMA((6,)),
-            pltpu.SemaphoreType.DMA((6,)),
-        ],
-        compiler_params=params(),
-        name="post",
-    )(away(r))
+    return edge(post_body, (ROWS, PAIRS * 384), r, "post")
 
 
 def whole(body, out, *args, scratch=(), name=None, far=False):
@@ -170,22 +162,32 @@
     )(*[near(a) for a in args])
 
 
-def dft_f_body(r_ref, b_hbm, g_hbm, o_ref, x_ref, b_ref, g_ref, sem):
+def dft_f_body(r_ref, b_hbm, g_hbm, o_ref, x_ref, w_ref, b_ref, g_ref, sem):
     load_b = pltpu.make_async_copy(b_hbm, b_ref, sem.at[0])
     load_g = pltpu.make_async_copy(g_hbm, g_ref, sem.at[1])
     load_b.start()
     load_g.start()
-    for blk in range(NA):
-        for k in range(SLOTS):
-            v = r_ref[blk, :, 384 * k:384 * k + 384]
+
+    def gather(to_ref, slots):
+        for blk in range(NA):
             row = 2 * LP * blk
-            x_ref[row:row + LP, C * k:C * k + C] = v[:, :C]
-            x_ref[row + LP:row + 2 * LP, C * k:C * k + C] = v[:, C:]
+            for end in (row + LP, row + 2 * LP):
+                to_ref[end - 16:end, :] = jnp.zeros((16, C * len(slots)), BF)
+            for i, k in enumerate(slots):
+                at = 272 * k
+                v = [r_ref[blk, at + 90 * t:at + 90 * t + 90, :] for t in range(3)]
+                to_ref[row:row + 90, C * i:C * i + C] = jnp.concatenate([v[0], v[1][:, :64]], 1)
+                to_ref[row + LP:row + LP + 90, C * i:C * i + C] = jnp.concatenate([v[1][:, 64:], v[2]], 1)
+
+    gather(x_ref, (0, 1, 2, 3))
     load_b.wait()
     y = dot(b_ref[...], x_ref[...], 1, 0).astype(BF)
+    gather(w_ref, (4, 5))
+    o_ref[:, :4, :768] = y.reshape(128, 4, 768)
+    y = dot(b_ref[...], w_ref[...], 1, 0).astype(BF)
     load_g.wait()
     o_ref[:, 4:, :] = g_ref[...]
-    o_ref[:, :4, :] = y.reshape(128, 4, W)
+    o_ref[:, :4, 768:] = y.reshape(128, 4, 384)
 
 
 def dft_f(r, bpt, wire_g):
@@ -195,7 +197,8 @@
         out_specs=VMEM,
         out_shape=pltpu.VMEM((128, 8, W), BF),
         scratch_shapes=[
-            pltpu.VMEM((1536, W), BF),
+            pltpu.VMEM((1536, 768), BF),
+            pltpu.VMEM((1536, 384), BF),
             pltpu.VMEM((512, 1536), BF),
             pltpu.VMEM((128, 4, W), BF),
             pltpu.SemaphoreType.DMA((2,)),
@@ -272,10 +275,10 @@
             m, r = j // 2, j % 2
             for t in range(48):
                 lane = C * r + 24 * a
-                z_ref[16 * j:16 * j + 16, 24 * t:24 * t + 24] = y_ref[m, 16 * t:16 * t + 16, lane:lane + 24]
+                z_ref[64 + 16 * j:80 + 16 * j, 24 * t:24 * t + 24] = y_ref[m, 16 * t:16 * t + 16, lane:lane + 24]
             for k in range(SLOTS):
                 row = 128 * k + 16 * a
-                z_ref[64 + 16 * j:80 + 16 * j, C * k:C * k + C] = y_ref[2 + m, row:row + 16, C * r:C * r + C]
+                z_ref[16 * j:16 * j + 16, C * k:C * k + C] = y_ref[2 + m, row:row + 16, C * r:C * r + C]
         o_ref[:, a, :, :] = swap_rows(z_ref[...], 8, NP).reshape(NP, 8, W)
 
 
@@ -285,7 +288,7 @@
 
 
 def idft_f_body(y_ref, b_ref, o_ref):
-    y = y_ref[:, :4, :].reshape(512, W)
+    y = y_ref[:, 4:, :].reshape(512, W)
     o_ref[...] = dot(y[:, :1080], b_ref[...], 0, 0).astype(BF)
 
 
@@ -294,16 +297,19 @@
 
 
 def idft_g_body(y_ref, b_ref, o_hbm, o_ref, sem):
-    y = y_ref[:, 4:, :].reshape(512, W)
+    y = y_ref[:, :4, :].reshape(512, W)
     stores = []
     for i in range(4):
         z = dot(b_ref[4 * LP * i:4 * LP * (i + 1), :], y, 1, 0).astype(BF)
         for half in range(2):
             row = 2 * LP * half
             for k in range(SLOTS):
-                e = z[row:row + LP, C * k:C * k + C]
-                o = z[row + LP:row + 2 * LP, C * k:C * k + C]
-                o_ref[2 * i + half, :, 384 * k:384 * k + 384] = jnp.concatenate([e, o], 1)
+                e = z[row:row + 90, C * k:C * k + C]
+                o = z[row + LP:row + LP + 90, C * k:C * k + C]
+                v = jnp.concatenate([e, o], 1)
+                for t in range(3):
+                    at = 272 * k + 90 * t
+                    o_ref[2 * i + half, at:at + 90, :] = v[:, 128 * t:128 * t + 128]
         part = pl.ds(2 * i, 2)
         stores.append(pltpu.make_async_copy(o_ref.at[part], o_hbm.at[part], sem.at[i]))
         stores[i].start()
@@ -316,8 +322,8 @@
         idft_g_body,
         in_specs=[VMEM, VMEM],
         out_specs=ANY,
-        out_shape=pltpu.HBM((NA, LP, 2304), BF),
-        scratch_shapes=[pltpu.VMEM((NA, LP, 2304), BF), pltpu.SemaphoreType.DMA((4,))],
+        out_shape=pltpu.HBM((NA, WIRE, 128), BF),
+        scratch_shapes=[pltpu.VMEM((NA, WIRE, 128), BF), pltpu.SemaphoreType.DMA((4,))],
         compiler_params=params(),
         name="idft_g",
     )(near(y), near(bp))

time: 235 us -> 231 us (0.983)
  waiting for transfers between devices: 54.9 us -> 50.7 us
    all_to_all x2, waiting for transfers between devices: 54.9 us -> 50.7 us  [over_azimuth(): return lax.all_to_all(x, 'azimuth', 0, 0)]
where the time goes in v5:
time: 231 us; the launch traced here: 230 us
  blocking collectives  114 us (49%)
  waiting for transfers between devices  50.7 us (22%)
  Pallas kernels  31 us (13%)
  local copies, waits for them, and re-layouts  18 us (8%)
  starting transfers between devices  11.3 us (5%)
  other arithmetic  4.37 us (2%)
    all_to_all x2, blocking collectives, over_all(): return lax.all_to_all(x, both, 0, 0)  77.3 us
    all_to_all x2, waiting for transfers between devices, over_azimuth(): return lax.all_to_all(x, 'azimuth', 0, 0)  50.7 us
    all_to_all x2, blocking collectives, over_polar(): return lax.all_to_all(x, 'polar', 0, 0)  36.6 us
    pallas_call x5, Pallas kernels, whole(): pl.pallas_call(body, in_specs=[VMEM] * len(args), out_specs=VMEM, out_sha...  17 us
    all_to_all x2, starting transfers between devices, over_azimuth(): return lax.all_to_all(x, 'azimuth', 0, 0)  11.3 us
    pallas_call x2, Pallas kernels, edge(): pl.pallas_call(body, in_specs=[ANY], out_specs=ANY, out_shape=pltpu.HBM(o...  6.02 us
    reshape x1, local copies, waits for them, and re-layouts, on_device(): cube = filter_weight.reshape(16, 2, C, C)  5.94 us
    unnamed x22, local copies, waits for them, and re-layouts  5.56 us
  transfers between devices with their start and end apart: 2, of which 2 were waited for; matrix products, arithmetic and copies ran while one was open for 7% of the time, Pallas kernels for 3%

profile of v5, /device:TPU:1, one launch (start us, length us, event | category | flops | bytes accessed | tf_op | source)
XLA Modules:
  0.0 230.2 jit_solution(9767378754511176400)
XLA Ops:
  0.6 3.0 %prep.1 = bf16[8,1632,128]{2,1,0:T(8,128)(2,1)} custom-call(bf16[45,34560]{1,0:T(8,128)(2,1)} %x_hbm.1), custom_call_target="tpu_custom_call" | custom-call | tf_op jit(solution)/shard_map/prep/pallas_call | solution.py:104
  3.6 6.8 %all-to-all-start = ((bf16[8,1632,128]{2,1,0:T(8,128)(2,1)}), bf16[8,1632,128]{2,1,0:T(8,128)(2,1)S(1)}, u32[]{:S(2)}, u32[]{:S(2)}) async-start(bf16[8,1632,128]{2,1,0:T(8,128)(2,1)} %prep.1), calls=%async_computation | async-start | bytes 6684672 | tf_op jit(solution)/shard_map/all_to_all | solution.py:354
  10.4 4.2 %constant_dynamic-slice_fusion = (bf16[720,2,256]{2,1,0:T(2,128)(2,1)S(1)}, bf16[720,2,256]{2,1,0:T(2,128)(2,1)S(1)}) fusion(bf16[720,16,256]{2,1,0:T(8,128)(2,1)} %param.11, s32[]{:T(128)S(6)} %select_n.4, bf16[720,16,256]{2,1,0:T(8,128)(2,1)} %param.10), kind=kLoop, calls=%fused_computation.3 | loop fusion | bytes 2949124 | tf_op jit(solution)/shard_map/dynamic_slice | solution.py:333
  14.7 0.1 copy.17
  14.8 0.1 copy.16
  14.9 0.9 pad.7.clone
  15.9 1.0 pad.8.clone
  16.8 5.9 %reshape.42 = bf16[16,2,192,192]{3,2,1,0:T(8,128)(2,1)} reshape(bf16[16,73728]{1,0:T(8,128)(2,1)} %param.12) | data formatting | bytes 4718592 | tf_op jit(solution)/shard_map/reshape | solution.py:364
  22.8 1.4 copy-done.2
  24.2 1.9 copy-done.5
  26.1 2.2 dft_g.1.g_hbm
  28.4 0.1 fusion
  28.5 0.3 slice_bitcast_fusion
  28.8 0.6 copy-done.4
  29.4 4.3 %maximum_maximum_fusion.k_ref = bf16[16,384,384]{2,1,0:T(8,128)(2,1)} fusion(bf16[16,192,192]{2,1,0:T(8,128)(2,1)S(1)} %get-tuple-element.21, bf16[16,192,192]{2,1,0:T(8,128)(2,1)S(1)} %fusion, bf16[16,192,192]{2,1,0:T(8,128)(2,1)S(1)} %get-tuple-element.20), kind=kLoop, calls=%fused_computation | loop fusion | flops 18874368 | bytes 8257536 | tf_op jit(solution)/shard_map/concatenate | solution.py:367
  33.7 16.3 %all-to-all-done.r_ref = bf16[8,1632,128]{2,1,0:T(8,128)(2,1)S(1)} async-done(((bf16[8,1632,128]{2,1,0:T(8,128)(2,1)}), bf16[8,1632,128]{2,1,0:T(8,128)(2,1)S(1)}, u32[]{:S(2)}, u32[]{:S(2)}) %all-to-all-start) | async-done | bytes 3342368 | tf_op jit(solution)/shard_map/all_to_all | solution.py:354
  49.9 4.6 %dft_f.1 = bf16[128,8,1152]{2,1,0:T(8,128)(2,1)S(1)} custom-call(bf16[8,1632,128]{2,1,0:T(8,128)(2,1)S(1)} %all-to-all-done.r_ref, bf16[512,1536]{1,0:T(8,128)(2,1)} %constant.19.clone.b_hbm, bf16[128,4,1152]{2,1,0:T(4,128)(2,1)} %copy-done.4), custom_call_target="tpu_custom_call" | custom-call | tf_op jit(solution)/shard_map/dft_f/pallas_call | solution.py:194
  54.6 40.8 %all_to_all.30 = bf16[128,8,1152]{2,1,0:T(8,128)(2,1)S(1)} all-to-all(bf16[128,8,1152]{2,1,0:T(8,128)(2,1)S(1)} %dft_f.1), channel_id=1, replica_groups=mesh['polar'=16,'azimuth'=8] {'polar','azimuth'}, dimensions={0} | all-to-all | bytes 4718592 | tf_op jit(solution)/shard_map/all_to_all | solution.py:348
  95.4 4.1 %leg.1 = bf16[256,1536]{1,0:T(8,128)(2,1)S(1)} custom-call(bf16[16,8,8,1152]{3,2,1,0:T(8,128)(2,1)S(1)} %bitcast.27, bf16[2,768,256]{2,1,0:T(8,128)(2,1)S(1)} %bitcast.28, bf16[2,768,256]{2,1,0:T(8,128)(2,1)S(1)} %bitcast.30), custom_call_target="tpu_custom_call" | custom-call | tf_op jit(solution)/shard_map/leg/pallas_call | solution.py:154
  99.5 18.8 %all_to_all.31.r_ref = bf16[16,16,1536]{2,1,0:T(8,128)(2,1)S(1)} all-to-all(bf16[16,16,1536]{2,1,0:T(8,128)(2,1)S(1)} %bitcast.34), channel_id=1, replica_groups=mesh['polar'=16,'azimuth'=8] {'polar'}, dimensions={0} | all-to-all | bytes 1572864 | tf_op jit(solution)/shard_map/all_to_all | solution.py:351
  118.3 2.9 %mix.1 = bf16[16,16,1536]{2,1,0:T(8,128)(2,1)S(1)} custom-call(bf16[16,16,1536]{2,1,0:T(8,128)(2,1)S(1)} %all_to_all.31.r_ref, bf16[16,384,384]{2,1,0:T(8,128)(2,1)S(1)} %bitcast.25), custom_call_target="tpu_custom_call" | custom-call | tf_op jit(solution)/shard_map/mix/pallas_call | solution.py:154
  121.2 17.8 %all_to_all.32 = bf16[16,16,1536]{2,1,0:T(8,128)(2,1)S(1)} all-to-all(bf16[16,16,1536]{2,1,0:T(8,128)(2,1)S(1)} %mix.1), channel_id=1, replica_groups=mesh['polar'=16,'azimuth'=8] {'polar'}, dimensions={0} | all-to-all | bytes 1572864 | tf_op jit(solution)/shard_map/all_to_all | solution.py:351
  139.0 4.1 %syn.1 = bf16[16,8,8,1152]{3,2,1,0:T(8,128)(2,1)S(1)} custom-call(bf16[256,1536]{1,0:T(8,128)(2,1)S(1)} %bitcast.33, bf16[2,768,256]{2,1,0:T(8,128)(2,1)S(1)} %bitcast.29, bf16[2,768,256]{2,1,0:T(8,128)(2,1)S(1)} %bitcast.31), custom_call_target="tpu_custom_call" | custom-call | tf_op jit(solution)/shard_map/syn/pallas_call | solution.py:154
  143.1 0.0 copy-start.6
  143.1 36.6 %all_to_all.33.y_ref = bf16[128,8,1152]{2,1,0:T(8,128)(2,1)S(1)} all-to-all(bf16[128,8,1152]{2,1,0:T(8,128)(2,1)S(1)} %bitcast.26), channel_id=1, replica_groups=mesh['polar'=16,'azimuth'=8] {'polar','azimuth'}, dimensions={0} | all-to-all | bytes 4718592 | tf_op jit(solution)/shard_map/all_to_all | solution.py:348
  179.7 3.3 %idft_g.1 = bf16[8,1632,128]{2,1,0:T(8,128)(2,1)} custom-call(bf16[128,8,1152]{2,1,0:T(8,128)(2,1)S(1)} %all_to_all.33.y_ref, bf16[1536,512]{1,0:T(8,128)(2,1)S(1)} %copy-done.6), custom_call_target="tpu_custom_call" | custom-call | tf_op jit(solution)/shard_map/idft_g/pallas_call | solution.py:321
  183.0 4.5 %all-to-all-start.5 = ((bf16[8,1632,128]{2,1,0:T(8,128)(2,1)}), bf16[8,1632,128]{2,1,0:T(8,128)(2,1)}, u32[]{:S(2)}, u32[]{:S(2)}) async-start(bf16[8,1632,128]{2,1,0:T(8,128)(2,1)} %idft_g.1), calls=%async_computation.5 | async-start | bytes 6684672 | tf_op jit(solution)/shard_map/all_to_all | solution.py:354
  187.5 0.0 copy-start.3
  187.5 1.4 copy-done.3
  188.9 3.7 %idft_f.1 = bf16[1080,1440]{1,0:T(8,128)(2,1)} custom-call(bf16[128,8,1152]{2,1,0:T(8,128)(2,1)S(1)} %all_to_all.33.y_ref, bf16[512,1440]{1,0:T(8,128)(2,1)S(1)} %copy-done.3), custom_call_target="tpu_custom_call" | custom-call | tf_op jit(solution)/shard_map/idft_f/pallas_call | solution.py:154
  192.6 34.4 %all-to-all-done.5.r_hbm = bf16[8,1632,128]{2,1,0:T(8,128)(2,1)} async-done(((bf16[8,1632,128]{2,1,0:T(8,128)(2,1)}), bf16[8,1632,128]{2,1,0:T(8,128)(2,1)}, u32[]{:S(2)}, u32[]{:S(2)}) %all-to-all-start.5) | async-done | bytes 3342368 | tf_op jit(solution)/shard_map/all_to_all | solution.py:354
  227.0 3.0 %post.1 = bf16[45,34560]{1,0:T(8,128)(2,1)} custom-call(bf16[8,1632,128]{2,1,0:T(8,128)(2,1)} %all-to-all-done.5.r_hbm), custom_call_target="tpu_custom_call" | custom-call | tf_op jit(solution)/shard_map/post/pallas_call | solution.py:104
  (15 shorter events, 0.0 us)
Async XLA Ops:
  3.6 46.3 %all-to-all-start = ((bf16[8,1632,128]{2,1,0:T(8,128)(2,1)}), bf16[8,1632,128]{2,1,0:T(8,128)(2,1)S(1)}, u32[]{:S(2)}, u32[]{:S(2)}) async-start(bf16[8,1632,128]{2,1,0:T(8,128)(2,1)} %prep.1), calls=%async_computation | async-start | bytes 6684672 | tf_op jit(solution)/shard_map/all_to_all | solution.py:354
  22.8 1.4 copy-start.2
  24.2 1.9 copy-start.5
  26.1 2.2 copy-start.7
  28.4 1.0 copy-start.4
  49.9 68.4 %slice-start = ((s8[4718592]{0:T(1024)(128)(4,1)}), s8[4194304]{0:T(1024)(128)(4,1)S(1)}, s32[]{:S(2)}) async-start(s8[4718592]{0:T(1024)(128)(4,1)} %bitcast.24), calls=%async_computation.6 | async-start | bytes 8388608
  54.6 40.8 %copy-start = (bf16[2,48,16,256]{3,2,1,0:T(8,128)(2,1)S(1)}, bf16[2,48,16,256]{3,2,1,0:T(8,128)(2,1)}, u32[]{:S(2)}) copy-start(bf16[2,48,16,256]{3,2,1,0:T(8,128)(2,1)} %pad.7.clone) | copy-start | bytes 2359300
  54.6 40.8 %copy-start.1 = (bf16[2,48,16,256]{3,2,1,0:T(8,128)(2,1)S(1)}, bf16[2,48,16,256]{3,2,1,0:T(8,128)(2,1)}, u32[]{:S(2)}) copy-start(bf16[2,48,16,256]{3,2,1,0:T(8,128)(2,1)} %pad.8.clone) | copy-start | bytes 2359300
  54.6 63.7 %slice-start.1 = ((s8[4718592]{0:T(1024)(128)(4,1)}), s8[524288]{0:T(1024)(128)(4,1)S(1)}, s32[]{:S(2)}) async-start(s8[4718592]{0:T(1024)(128)(4,1)} %bitcast.24), calls=%async_computation.7 | async-start | bytes 1048576
  143.1 36.6 %copy-start.6 = (bf16[1536,512]{1,0:T(8,128)(2,1)S(1)}, bf16[1536,512]{1,0:T(8,128)(2,1)}, u32[]{:S(2)}) copy-start(bf16[1536,512]{1,0:T(8,128)(2,1)} %constant.20.clone.b_ref) | copy-start | bytes 4718596
  183.0 44.0 %all-to-all-start.5 = ((bf16[8,1632,128]{2,1,0:T(8,128)(2,1)}), bf16[8,1632,128]{2,1,0:T(8,128)(2,1)}, u32[]{:S(2)}, u32[]{:S(2)}) async-start(bf16[8,1632,128]{2,1,0:T(8,128)(2,1)} %idft_g.1), calls=%async_computation.5 | async-start | bytes 6684672 | tf_op jit(solution)/shard_map/all_to_all | solution.py:354
  187.5 1.4 copy-start.3

commit v6 on v5

--- a/solution.py
+++ b/solution.py
@@ -166,7 +166,6 @@
     load_b = pltpu.make_async_copy(b_hbm, b_ref, sem.at[0])
     load_g = pltpu.make_async_copy(g_hbm, g_ref, sem.at[1])
     load_b.start()
-    load_g.start()
 
     def gather(to_ref, slots):
         for blk in range(NA):
@@ -181,6 +180,7 @@
 
     gather(x_ref, (0, 1, 2, 3))
     load_b.wait()
+    load_g.start()
     y = dot(b_ref[...], x_ref[...], 1, 0).astype(BF)
     gather(w_ref, (4, 5))
     o_ref[:, :4, :768] = y.reshape(128, 4, 768)
@@ -226,25 +226,28 @@
     return dot(perm, x, 1, 0).astype(BF)
 
 
-def leg_body(r_ref, pf_ref, pi_ref, o_ref, s_ref, t_ref):
+def leg_body(r_ref, pf_ref, pi_ref, o_ref, v_ref, *built):
     for a in range(NA):
-        v = swap_rows(r_ref[:, a, :, :].reshape(128, W), NP, 8)
-        for j in range(4):
-            m, r = j // 2, j % 2
-            for k in range(SLOTS):
-                row = 128 * k + 16 * a
-                s_ref[m, row:row + 16, C * r:C * r + C] = v[16 * j:16 * j + 16, C * k:C * k + C]
-            for t in range(48):
-                lane = C * r + 24 * a
-                t_ref[m, 16 * t:16 * t + 16, lane:lane + 24] = v[64 + 16 * j:80 + 16 * j, 24 * t:24 * t + 24]
+        v_ref[a] = swap_rows(r_ref[:, a, :, :].reshape(128, W), NP, 8)
     for m in range(2):
-        o_ref[:, 384 * m:384 * m + 384] = dot(pf_ref[m], s_ref[m], 0, 0).astype(BF)
-        o_ref[:, 768 + 384 * m:768 + 384 * m + 384] = dot(pi_ref[m], t_ref[m], 0, 0).astype(BF)
+        s_ref, t_ref = built[2 * m], built[2 * m + 1]
+        for a in range(NA):
+            for r in range(2):
+                j = 2 * m + r
+                for k in range(SLOTS):
+                    row = 128 * k + 16 * a
+                    s_ref[row:row + 16, C * r:C * r + C] = v_ref[a, 16 * j:16 * j + 16, C * k:C * k + C]
+                for t in range(48):
+                    lane = C * r + 24 * a
+                    t_ref[16 * t:16 * t + 16, lane:lane + 24] = v_ref[a, 64 + 16 * j:80 + 16 * j, 24 * t:24 * t + 24]
+        o_ref[:, 384 * m:384 * m + 384] = dot(pf_ref[m], s_ref[...], 0, 0).astype(BF)
+        o_ref[:, 768 + 384 * m:768 + 384 * m + 384] = dot(pi_ref[m], t_ref[...], 0, 0).astype(BF)
 
 
 def leg(r, pf, pi):
     r = r.reshape(NP, NA, 8, W)
-    return whole(leg_body, (DEG, 1536), r, pf, pi, scratch=[pltpu.VMEM((2, 768, 384), BF)] * 2, name="leg")
+    scratch = [pltpu.VMEM((NA, 128, W), BF)] + [pltpu.VMEM((768, 384), BF)] * 4
+    return whole(leg_body, (DEG, 1536), r, pf, pi, scratch=scratch, name="leg")
 
 
 def mix_body(r_ref, k_ref, o_ref, s_ref):
@@ -266,24 +269,26 @@
     return whole(mix_body, (16, 16, 1536), r, k, scratch=[pltpu.VMEM((256, 1536), BF)], name="mix")
 
 
-def syn_body(x_ref, pf_ref, pi_ref, o_ref, y_ref, z_ref):
+def syn_body(x_ref, pf_ref, pi_ref, o_ref, z_ref, *parts):
     for m in range(2):
-        y_ref[m] = dot(pi_ref[m], x_ref[:, 384 * m:384 * m + 384], 1, 0).astype(BF)
-        y_ref[2 + m] = dot(pf_ref[m], x_ref[:, 768 + 384 * m:768 + 384 * m + 384], 1, 0).astype(BF)
+        f_ref, g_ref = parts[2 * m], parts[2 * m + 1]
+        f_ref[...] = dot(pi_ref[m], x_ref[:, 384 * m:384 * m + 384], 1, 0).astype(BF)
+        g_ref[...] = dot(pf_ref[m], x_ref[:, 768 + 384 * m:768 + 384 * m + 384], 1, 0).astype(BF)
+        for a in range(NA):
+            for r in range(2):
+                j = 2 * m + r
+                for t in range(48):
+                    lane = C * r + 24 * a
+                    z_ref[a, 64 + 16 * j:80 + 16 * j, 24 * t:24 * t + 24] = f_ref[16 * t:16 * t + 16, lane:lane + 24]
+                for k in range(SLOTS):
+                    row = 128 * k + 16 * a
+                    z_ref[a, 16 * j:16 * j + 16, C * k:C * k + C] = g_ref[row:row + 16, C * r:C * r + C]
     for a in range(NA):
-        for j in range(4):
-            m, r = j // 2, j % 2
-            for t in range(48):
-                lane = C * r + 24 * a
-                z_ref[64 + 16 * j:80 + 16 * j, 24 * t:24 * t + 24] = y_ref[m, 16 * t:16 * t + 16, lane:lane + 24]
-            for k in range(SLOTS):
-                row = 128 * k + 16 * a
-                z_ref[16 * j:16 * j + 16, C * k:C * k + C] = y_ref[2 + m, row:row + 16, C * r:C * r + C]
-        o_ref[:, a, :, :] = swap_rows(z_ref[...], 8, NP).reshape(NP, 8, W)
+        o_ref[:, a, :, :] = swap_rows(z_ref[a], 8, NP).reshape(NP, 8, W)
 
 
 def syn(x, pf, pi):
-    scratch = [pltpu.VMEM((4, 768, 384), BF), pltpu.VMEM((128, W), BF)]
+    scratch = [pltpu.VMEM((NA, 128, W), BF)] + [pltpu.VMEM((768, 384), BF)] * 4
     return whole(syn_body, (NP, NA, 8, W), x, pf, pi, scratch=scratch, name="syn").reshape(128, 8, W)
 
 
@@ -299,20 +304,17 @@
 def idft_g_body(y_ref, b_ref, o_hbm, o_ref, sem):
     y = y_ref[:, :4, :].reshape(512, W)
     stores = []
-    for i in range(4):
-        z = dot(b_ref[4 * LP * i:4 * LP * (i + 1), :], y, 1, 0).astype(BF)
-        for half in range(2):
-            row = 2 * LP * half
-            for k in range(SLOTS):
-                e = z[row:row + 90, C * k:C * k + C]
-                o = z[row + LP:row + LP + 90, C * k:C * k + C]
-                v = jnp.concatenate([e, o], 1)
-                for t in range(3):
-                    at = 272 * k + 90 * t
-                    o_ref[2 * i + half, at:at + 90, :] = v[:, 128 * t:128 * t + 128]
-        part = pl.ds(2 * i, 2)
-        stores.append(pltpu.make_async_copy(o_ref.at[part], o_hbm.at[part], sem.at[i]))
-        stores[i].start()
+    for blk in range(NA):
+        z = dot(b_ref[2 * LP * blk:2 * LP * (blk + 1), :], y, 1, 0).astype(BF)
+        for k in range(SLOTS):
+            e = z[:90, C * k:C * k + C]
+            o = z[LP:LP + 90, C * k:C * k + C]
+            v = jnp.concatenate([e, o], 1)
+            for t in range(3):
+                at = 272 * k + 90 * t
+                o_ref[blk, at:at + 90, :] = v[:, 128 * t:128 * t + 128]
+        stores.append(pltpu.make_async_copy(o_ref.at[blk], o_hbm.at[blk], sem.at[blk]))
+        stores[blk].start()
     for copy in stores:
         copy.wait()
 
@@ -323,7 +325,7 @@
         in_specs=[VMEM, VMEM],
         out_specs=ANY,
         out_shape=pltpu.HBM((NA, WIRE, 128), BF),
-        scratch_shapes=[pltpu.VMEM((NA, WIRE, 128), BF), pltpu.SemaphoreType.DMA((4,))],
+        scratch_shapes=[pltpu.VMEM((NA, WIRE, 128), BF), pltpu.SemaphoreType.DMA((NA,))],
         compiler_params=params(),
         name="idft_g",
     )(near(y), near(bp))

time: 231 us -> 231 us (level)
  no operation moved by 1% of the time
where the time goes in v6:
time: 231 us
  blocking collectives  114 us (49%)
  waiting for transfers between devices  50.7 us (22%)
  Pallas kernels  31.5 us (14%)
  local copies, waits for them, and re-layouts  18 us (8%)
  starting transfers between devices  11.3 us (5%)
  other arithmetic  4.37 us (2%)
    all_to_all x2, blocking collectives, over_all(): return lax.all_to_all(x, both, 0, 0)  77.4 us
    all_to_all x2, waiting for transfers between devices, over_azimuth(): return lax.all_to_all(x, 'azimuth', 0, 0)  50.7 us
    all_to_all x2, blocking collectives, over_polar(): return lax.all_to_all(x, 'polar', 0, 0)  36.6 us
    pallas_call x5, Pallas kernels, whole(): pl.pallas_call(body, in_specs=[VMEM] * len(args), out_specs=VMEM, out_sha...  16.8 us
    all_to_all x2, starting transfers between devices, over_azimuth(): return lax.all_to_all(x, 'azimuth', 0, 0)  11.3 us
    pallas_call x2, Pallas kernels, edge(): pl.pallas_call(body, in_specs=[ANY], out_specs=ANY, out_shape=pltpu.HBM(o...  6.02 us
    reshape x1, local copies, waits for them, and re-layouts, on_device(): cube = filter_weight.reshape(16, 2, C, C)  5.94 us
    unnamed x22, local copies, waits for them, and re-layouts  5.56 us
  transfers between devices with their start and end apart: 2, of which 2 were waited for; matrix products, arithmetic and copies ran while one was open for 7% of the time, Pallas kernels for 3%

profile of v6, /device:TPU:1, one launch (start us, length us, event | category | flops | bytes accessed | tf_op | source)
XLA Modules:
  0.0 230.7 jit_solution(14736054596160470557)
XLA Ops:
  0.6 3.0 %prep.1 = bf16[8,1632,128]{2,1,0:T(8,128)(2,1)} custom-call(bf16[45,34560]{1,0:T(8,128)(2,1)} %x_hbm.1), custom_call_target="tpu_custom_call" | custom-call | tf_op jit(solution)/shard_map/prep/pallas_call | solution.py:104
  3.6 6.8 %all-to-all-start = ((bf16[8,1632,128]{2,1,0:T(8,128)(2,1)}), bf16[8,1632,128]{2,1,0:T(8,128)(2,1)S(1)}, u32[]{:S(2)}, u32[]{:S(2)}) async-start(bf16[8,1632,128]{2,1,0:T(8,128)(2,1)} %prep.1), calls=%async_computation | async-start | bytes 6684672 | tf_op jit(solution)/shard_map/all_to_all | solution.py:356
  10.4 4.2 %constant_dynamic-slice_fusion = (bf16[720,2,256]{2,1,0:T(2,128)(2,1)S(1)}, bf16[720,2,256]{2,1,0:T(2,128)(2,1)S(1)}) fusion(bf16[720,16,256]{2,1,0:T(8,128)(2,1)} %param.11, s32[]{:T(128)S(6)} %select_n.4, bf16[720,16,256]{2,1,0:T(8,128)(2,1)} %param.10), kind=kLoop, calls=%fused_computation.3 | loop fusion | bytes 2949124 | tf_op jit(solution)/shard_map/dynamic_slice | solution.py:335
  14.7 0.1 copy.17
  14.8 0.1 copy.16
  14.9 0.9 pad.7.clone
  15.9 1.0 pad.8.clone
  16.8 5.9 %reshape.42 = bf16[16,2,192,192]{3,2,1,0:T(8,128)(2,1)} reshape(bf16[16,73728]{1,0:T(8,128)(2,1)} %param.12) | data formatting | bytes 4718592 | tf_op jit(solution)/shard_map/reshape | solution.py:366
  22.8 1.4 copy-done.2
  24.2 1.9 copy-done.5
  26.1 2.2 dft_g.1.g_hbm
  28.4 0.1 fusion
  28.5 0.3 slice_bitcast_fusion
  28.8 0.6 copy-done.4
  29.4 4.3 %maximum_maximum_fusion.k_ref = bf16[16,384,384]{2,1,0:T(8,128)(2,1)} fusion(bf16[16,192,192]{2,1,0:T(8,128)(2,1)S(1)} %get-tuple-element.21, bf16[16,192,192]{2,1,0:T(8,128)(2,1)S(1)} %fusion, bf16[16,192,192]{2,1,0:T(8,128)(2,1)S(1)} %get-tuple-element.20), kind=kLoop, calls=%fused_computation | loop fusion | flops 18874368 | bytes 8257536 | tf_op jit(solution)/shard_map/concatenate | solution.py:369
  33.7 16.3 %all-to-all-done.r_ref = bf16[8,1632,128]{2,1,0:T(8,128)(2,1)S(1)} async-done(((bf16[8,1632,128]{2,1,0:T(8,128)(2,1)}), bf16[8,1632,128]{2,1,0:T(8,128)(2,1)S(1)}, u32[]{:S(2)}, u32[]{:S(2)}) %all-to-all-start) | async-done | bytes 3342368 | tf_op jit(solution)/shard_map/all_to_all | solution.py:356
  49.9 5.4 %dft_f.1 = bf16[128,8,1152]{2,1,0:T(8,128)(2,1)S(1)} custom-call(bf16[8,1632,128]{2,1,0:T(8,128)(2,1)S(1)} %all-to-all-done.r_ref, bf16[512,1536]{1,0:T(8,128)(2,1)} %constant.19.clone.b_hbm, bf16[128,4,1152]{2,1,0:T(4,128)(2,1)} %copy-done.4), custom_call_target="tpu_custom_call" | custom-call | tf_op jit(solution)/shard_map/dft_f/pallas_call | solution.py:194
  55.4 40.8 %all_to_all.30 = bf16[128,8,1152]{2,1,0:T(8,128)(2,1)S(1)} all-to-all(bf16[128,8,1152]{2,1,0:T(8,128)(2,1)S(1)} %dft_f.1), channel_id=1, replica_groups=mesh['polar'=16,'azimuth'=8] {'polar','azimuth'}, dimensions={0} | all-to-all | bytes 4718592 | tf_op jit(solution)/shard_map/all_to_all | solution.py:350
  96.2 4.1 %leg.1 = bf16[256,1536]{1,0:T(8,128)(2,1)S(1)} custom-call(bf16[16,8,8,1152]{3,2,1,0:T(8,128)(2,1)S(1)} %bitcast.27, bf16[2,768,256]{2,1,0:T(8,128)(2,1)S(1)} %bitcast.28, bf16[2,768,256]{2,1,0:T(8,128)(2,1)S(1)} %bitcast.30), custom_call_target="tpu_custom_call" | custom-call | tf_op jit(solution)/shard_map/leg/pallas_call | solution.py:154
  100.2 18.8 %all_to_all.31.r_ref = bf16[16,16,1536]{2,1,0:T(8,128)(2,1)S(1)} all-to-all(bf16[16,16,1536]{2,1,0:T(8,128)(2,1)S(1)} %bitcast.34), channel_id=1, replica_groups=mesh['polar'=16,'azimuth'=8] {'polar'}, dimensions={0} | all-to-all | bytes 1572864 | tf_op jit(solution)/shard_map/all_to_all | solution.py:353
  119.1 2.9 %mix.1 = bf16[16,16,1536]{2,1,0:T(8,128)(2,1)S(1)} custom-call(bf16[16,16,1536]{2,1,0:T(8,128)(2,1)S(1)} %all_to_all.31.r_ref, bf16[16,384,384]{2,1,0:T(8,128)(2,1)S(1)} %bitcast.25), custom_call_target="tpu_custom_call" | custom-call | tf_op jit(solution)/shard_map/mix/pallas_call | solution.py:154
  121.9 17.8 %all_to_all.32 = bf16[16,16,1536]{2,1,0:T(8,128)(2,1)S(1)} all-to-all(bf16[16,16,1536]{2,1,0:T(8,128)(2,1)S(1)} %mix.1), channel_id=1, replica_groups=mesh['polar'=16,'azimuth'=8] {'polar'}, dimensions={0} | all-to-all | bytes 1572864 | tf_op jit(solution)/shard_map/all_to_all | solution.py:353
  139.7 3.9 %syn.1 = bf16[16,8,8,1152]{3,2,1,0:T(8,128)(2,1)S(1)} custom-call(bf16[256,1536]{1,0:T(8,128)(2,1)S(1)} %bitcast.33, bf16[2,768,256]{2,1,0:T(8,128)(2,1)S(1)} %bitcast.29, bf16[2,768,256]{2,1,0:T(8,128)(2,1)S(1)} %bitcast.31), custom_call_target="tpu_custom_call" | custom-call | tf_op jit(solution)/shard_map/syn/pallas_call | solution.py:154
  143.6 0.0 copy-start.6
  143.7 36.6 %all_to_all.33.y_ref = bf16[128,8,1152]{2,1,0:T(8,128)(2,1)S(1)} all-to-all(bf16[128,8,1152]{2,1,0:T(8,128)(2,1)S(1)} %bitcast.26), channel_id=1, replica_groups=mesh['polar'=16,'azimuth'=8] {'polar','azimuth'}, dimensions={0} | all-to-all | bytes 4718592 | tf_op jit(solution)/shard_map/all_to_all | solution.py:350
  180.3 3.3 %idft_g.1 = bf16[8,1632,128]{2,1,0:T(8,128)(2,1)} custom-call(bf16[128,8,1152]{2,1,0:T(8,128)(2,1)S(1)} %all_to_all.33.y_ref, bf16[1536,512]{1,0:T(8,128)(2,1)S(1)} %copy-done.6), custom_call_target="tpu_custom_call" | custom-call | tf_op jit(solution)/shard_map/idft_g/pallas_call | solution.py:323
  183.6 4.5 %all-to-all-start.5 = ((bf16[8,1632,128]{2,1,0:T(8,128)(2,1)}), bf16[8,1632,128]{2,1,0:T(8,128)(2,1)}, u32[]{:S(2)}, u32[]{:S(2)}) async-start(bf16[8,1632,128]{2,1,0:T(8,128)(2,1)} %idft_g.1), calls=%async_computation.5 | async-start | bytes 6684672 | tf_op jit(solution)/shard_map/all_to_all | solution.py:356
  188.1 0.0 copy-start.3
  188.1 1.4 copy-done.3
  189.5 3.7 %idft_f.1 = bf16[1080,1440]{1,0:T(8,128)(2,1)} custom-call(bf16[128,8,1152]{2,1,0:T(8,128)(2,1)S(1)} %all_to_all.33.y_ref, bf16[512,1440]{1,0:T(8,128)(2,1)S(1)} %copy-done.3), custom_call_target="tpu_custom_call" | custom-call | tf_op jit(solution)/shard_map/idft_f/pallas_call | solution.py:154
  193.2 34.4 %all-to-all-done.5.r_hbm = bf16[8,1632,128]{2,1,0:T(8,128)(2,1)} async-done(((bf16[8,1632,128]{2,1,0:T(8,128)(2,1)}), bf16[8,1632,128]{2,1,0:T(8,128)(2,1)}, u32[]{:S(2)}, u32[]{:S(2)}) %all-to-all-start.5) | async-done | bytes 3342368 | tf_op jit(solution)/shard_map/all_to_all | solution.py:356
  227.5 3.0 %post.1 = bf16[45,34560]{1,0:T(8,128)(2,1)} custom-call(bf16[8,1632,128]{2,1,0:T(8,128)(2,1)} %all-to-all-done.5.r_hbm), custom_call_target="tpu_custom_call" | custom-call | tf_op jit(solution)/shard_map/post/pallas_call | solution.py:104
  (15 shorter events, 0.0 us)
Async XLA Ops:
  3.6 46.3 %all-to-all-start = ((bf16[8,1632,128]{2,1,0:T(8,128)(2,1)}), bf16[8,1632,128]{2,1,0:T(8,128)(2,1)S(1)}, u32[]{:S(2)}, u32[]{:S(2)}) async-start(bf16[8,1632,128]{2,1,0:T(8,128)(2,1)} %prep.1), calls=%async_computation | async-start | bytes 6684672 | tf_op jit(solution)/shard_map/all_to_all | solution.py:356
  22.8 1.4 copy-start.2
  24.2 1.9 copy-start.5
  26.1 2.2 copy-start.7
  28.4 1.0 copy-start.4
  49.9 69.1 %slice-start = ((s8[4718592]{0:T(1024)(128)(4,1)}), s8[4194304]{0:T(1024)(128)(4,1)S(1)}, s32[]{:S(2)}) async-start(s8[4718592]{0:T(1024)(128)(4,1)} %bitcast.24), calls=%async_computation.6 | async-start | bytes 8388608
  55.4 40.8 %copy-start = (bf16[2,48,16,256]{3,2,1,0:T(8,128)(2,1)S(1)}, bf16[2,48,16,256]{3,2,1,0:T(8,128)(2,1)}, u32[]{:S(2)}) copy-start(bf16[2,48,16,256]{3,2,1,0:T(8,128)(2,1)} %pad.7.clone) | copy-start | bytes 2359300
  55.4 40.8 %copy-start.1 = (bf16[2,48,16,256]{3,2,1,0:T(8,128)(2,1)S(1)}, bf16[2,48,16,256]{3,2,1,0:T(8,128)(2,1)}, u32[]{:S(2)}) copy-start(bf16[2,48,16,256]{3,2,1,0:T(8,128)(2,1)} %pad.8.clone) | copy-start | bytes 2359300
  55.4 63.7 %slice-start.1 = ((s8[4718592]{0:T(1024)(128)(4,1)}), s8[524288]{0:T(1024)(128)(4,1)S(1)}, s32[]{:S(2)}) async-start(s8[4718592]{0:T(1024)(128)(4,1)} %bitcast.24), calls=%async_computation.7 | async-start | bytes 1048576
  143.6 36.6 %copy-start.6 = (bf16[1536,512]{1,0:T(8,128)(2,1)S(1)}, bf16[1536,512]{1,0:T(8,128)(2,1)}, u32[]{:S(2)}) copy-start(bf16[1536,512]{1,0:T(8,128)(2,1)} %constant.20.clone.b_ref) | copy-start | bytes 4718596
  183.6 44.0 %all-to-all-start.5 = ((bf16[8,1632,128]{2,1,0:T(8,128)(2,1)}), bf16[8,1632,128]{2,1,0:T(8,128)(2,1)}, u32[]{:S(2)}, u32[]{:S(2)}) async-start(bf16[8,1632,128]{2,1,0:T(8,128)(2,1)} %idft_g.1), calls=%async_computation.5 | async-start | bytes 6684672 | tf_op jit(solution)/shard_map/all_to_all | solution.py:356
  188.1 1.4 copy-start.3
